TPU v7x, 32 devices: a whole 2x2x4 slice. The times are simulated.
32 devices in a mesh: axial: 8 (over y, x, core), azim: 4 (over z).
Axes of the slice: x: 2, y: 2, z: 4, core: 2. Of those that a mesh axis runs over, the one named last changes fastest.
Arguments:
- state: float32 [5, 16, 1024, 96], P(None, 'axial', 'azim'), as said below
- start: float32 [5, 16, 1024, 96], P(None, 'axial', 'azim'), as said below
- modes: int32 [64], replicated, may hold values from 1 to 512, as said below
Outputs:
- section: float32 [5, 16, 1024, 96], P(None, 'axial', 'azim')
Inputs may be any that keep to these rules, and one draw needn't show every extreme that they name: Cycle j keeps the modes 0 to modes[j] - 1; modes[j] lies between 8 * (j + 1) and 2 * 8 * (j + 1), capped at 512, which the last cycle reaches. `state`: the density (field 0) lies between 0.85 and 1.15. `start`: the density (field 0) lies between 0.85 and 1.15.
All inputs are finite; a program needn't handle non-finite values.
Results may differ from a plain program's by a relative error of at most 0.00005.
Values sent between devices are 32-bit elements; how exact they have to be, the bound alone decides.
A program may use at most 64 MiB of HBM per device.

v0:
```python
import math

import jax
import jax.numpy as jnp
from jax import lax
from jax.sharding import PartitionSpec as P

NTH = 1024
NIN = 64


GAMMA = 1.4
STEP_DT = 0.05


def swapped(value, axis, bit):
    return lax.ppermute(value, axis, [(i, i ^ 1 << bit) for i in range(lax.axis_size(axis))])


def with_halo(cells, sides, width):
    for axis, dim in sides:
        count = lax.axis_size(axis)
        head = lax.slice_in_dim(cells, 0, width, axis=dim)
        tail = lax.slice_in_dim(cells, cells.shape[dim] - width, cells.shape[dim], axis=dim)
        cells = jnp.concatenate(
            [
                lax.ppermute(tail, axis, [(i, (i + 1) % count) for i in range(count)]),
                cells,
                lax.ppermute(head, axis, [((i + 1) % count, i) for i in range(count)]),
            ],
            axis=dim,
        )
    return cells


def central_diff(values, dimension):
    length = values.shape[dimension] - 4

    def part_at(offset):
        return lax.slice_in_dim(values, offset, offset + length, axis=dimension)

    return (8.0 * (part_at(3) - part_at(1)) - (part_at(4) - part_at(0))) / 12.0


def pressure_of(values, inverse):
    kinetic = (values[1] * values[1] + values[2] * values[2] + values[3] * values[3]) * inverse
    return (GAMMA - 1.0) * (values[4] - 0.5 * kinetic)


def flux_along(values, direction):
    inverse = 1.0 / values[0]
    velocity = values[direction] * inverse
    pressure = pressure_of(values, inverse)
    components = [
        values[direction],
        values[1] * velocity,
        values[2] * velocity,
        values[3] * velocity,
        (values[4] + pressure) * velocity,
    ]
    components[direction] = components[direction] + pressure
    return jnp.stack(components)


def rates_of(padded, dtheta):
    axial_cells = padded[:, :, 2:-2, 2:-2]
    azimuth_cells = padded[:, 2:-2, :, 2:-2]
    radial_cells = padded[:, 2:-2, 2:-2, :]
    centre = padded[:, 2:-2, 2:-2, 2:-2]
    radius_all = jnp.arange(padded.shape[3], dtype=jnp.float32) - 1.5
    inv_radius = 1.0 / radius_all[2:-2]
    axial_term = central_diff(flux_along(axial_cells, 1), 1)
    radial_term = central_diff(flux_along(radial_cells, 2) * radius_all, 3) * inv_radius
    azimuth_term = central_diff(flux_along(azimuth_cells, 3), 2) * (inv_radius / dtheta)
    inverse = 1.0 / centre[0]
    pressure = pressure_of(centre, inverse)
    source_radial = (centre[3] * centre[3] * inverse + pressure) * inv_radius
    source_azimuth = -(centre[2] * centre[3] * inverse) * inv_radius
    totals = -(axial_term + radial_term + azimuth_term)
    return jnp.stack(
        [totals[0], totals[1], totals[2] + source_radial, totals[3] + source_azimuth, totals[4]]
    )


def radial_extend(haloed, partner):
    signs = jnp.array([1.0, 1.0, -1.0, -1.0, 1.0], dtype=jnp.float32).reshape(5, 1, 1, 1)
    ghost = jnp.flip(partner, 3) * signs
    rim_axial = (haloed.shape[1] - ghost.shape[1]) // 2
    rim_theta = (haloed.shape[2] - ghost.shape[2]) // 2
    ghost = jnp.pad(ghost, ((0, 0), (rim_axial, rim_axial), (rim_theta, rim_theta), (0, 0)))
    outer_cycles = jnp.repeat(haloed[..., -1:], 2, axis=3)
    return jnp.concatenate([ghost, haloed, outer_cycles], axis=3)


def fourier_tables():
    half_modes = NTH // 2
    mode_block = min(128, half_modes)
    block_count = half_modes // mode_block
    wavenumbers = jnp.arange(half_modes, dtype=jnp.int32)
    cell_numbers = jnp.arange(NTH, dtype=jnp.int32)
    phase_index = cell_numbers[:, None] * wavenumbers[None, :] % NTH
    angles = phase_index.astype(jnp.float32) * (2.0 * math.pi / NTH)
    cosines = jnp.cos(angles).reshape(NTH, block_count, mode_block).transpose(1, 0, 2)
    sines = jnp.sin(angles).reshape(NTH, block_count, mode_block).transpose(1, 0, 2)
    tables = jnp.concatenate([cosines, sines], axis=2)
    weights = (
        jnp.where(wavenumbers == 0, 1.0 / NTH, 2.0 / NTH)
        .astype(jnp.float32)
        .reshape(block_count, mode_block)
    )
    return (tables, weights, wavenumbers.reshape(block_count, mode_block), mode_block)


def truncate_cycles(slab, local_modes, tables, weights, wave_blocks, mode_block):

    def one_cycle(cycle_index, result):
        cycle_values = lax.dynamic_index_in_dim(slab, cycle_index, 1, keepdims=False)
        mode_count = lax.dynamic_index_in_dim(local_modes, cycle_index, 0, keepdims=False)
        used_blocks = (mode_count + mode_block - 1) // mode_block

        def one_block(block_index, series_sum):
            basis_block = lax.dynamic_index_in_dim(tables, block_index, 0, keepdims=False)
            coeffs = jnp.dot(cycle_values, basis_block, precision=lax.Precision.HIGHEST)
            block_waves = lax.dynamic_index_in_dim(wave_blocks, block_index, 0, keepdims=False)
            block_weights = lax.dynamic_index_in_dim(weights, block_index, 0, keepdims=False)
            kept_weights = jnp.where(block_waves < mode_count, block_weights, 0.0)
            scaled = coeffs * jnp.concatenate([kept_weights, kept_weights])
            return series_sum + lax.dot_general(
                scaled, basis_block, (((1,), (1,)), ((), ())), precision=lax.Precision.HIGHEST
            )

        series = lax.fori_loop(
            0, used_blocks, one_block, jnp.zeros(cycle_values.shape, jnp.float32)
        )
        return lax.dynamic_update_index_in_dim(result, series, cycle_index, 1)

    return lax.fori_loop(0, slab.shape[1], one_cycle, jnp.zeros(slab.shape, jnp.float32))


def shards(state, start, modes):
    field_count, axial_local, theta_local, cycle_total = state.shape
    azim_size = lax.axis_size("azim")
    azim_index = lax.axis_index("azim")
    cycles_local = NIN // azim_size
    item_count = field_count * axial_local
    tables, weights, wave_blocks, mode_block = fourier_tables()
    inner = state[..., :NIN].transpose(0, 1, 3, 2).reshape(item_count, NIN, theta_local)
    local_modes = lax.dynamic_slice_in_dim(modes, azim_index * cycles_local, cycles_local)
    smoothed = truncate_cycles(
        lax.all_to_all(inner, "azim", split_axis=1, concat_axis=2, tiled=True),
        local_modes,
        tables,
        weights,
        wave_blocks,
        mode_block,
    )
    exchanged = lax.all_to_all(smoothed, "azim", split_axis=2, concat_axis=1, tiled=True)
    smooth_inner = exchanged.reshape(field_count, axial_local, NIN, theta_local).transpose(
        0, 1, 3, 2
    )
    smoothed_state = jnp.concatenate([smooth_inner, state[..., NIN:]], axis=3)
    partner = swapped(smoothed_state[..., :2], "azim", azim_size.bit_length() - 2)
    haloed = with_halo(smoothed_state, (("axial", 1), ("azim", 2)), 2)
    padded = radial_extend(haloed, partner)
    rate = rates_of(padded, 2.0 * math.pi / NTH)
    return start + STEP_DT * rate


def solution(mesh):
    in_specs = (P(None, "axial", "azim", None), P(None, "axial", "azim", None), P())
    out_specs = P(None, "axial", "azim", None)
    return jax.shard_map(shards, mesh=mesh, in_specs=in_specs, out_specs=out_specs, check_vma=False)
```

profile of v0, /device:TPU:0, one launch (start us, length us, event | category | flops | bytes accessed | tf_op | source)
XLA Modules:
  0.0 475.3 jit_solution(14893907723052022930)
XLA Ops:
  2.6 6.3 %all-to-all-start = ((f32[10,64,256]{2,0,1:T(8,128)}), f32[10,64,256]{2,0,1:T(8,128)S(1)}, u32[]{:S(2)}, u32[]{:S(2)}) async-start(f32[10,64,256]{2,0,1:T(8,128)} %copy.27), calls=%async_computation | async-start | bytes 2097152 | tf_op jit(solution)/shard_map/all_to_all | solution.py:150
  9.0 8.1 %fusion.19 = (f32[4,1024,128]{2,1,0:T(8,128)S(1)}, f32[4,1024,128]{2,1,0:T(8,128)S(1)}) fusion(s32[4,128]{1,0:T(4,128)S(1)} %multiply_add_fusion.1), kind=kLoop, calls=%fused_computation.45 | loop fusion | flops 7340032 | bytes 4196352 | tf_op jit(solution)/shard_map/cos | solution.py:103
  17.1 2.2 pad_maximum_fusion.1
  19.4 15.3 %all-to-all-done = f32[10,64,256]{2,0,1:T(8,128)S(1)} async-done(((f32[10,64,256]{2,0,1:T(8,128)}), f32[10,64,256]{2,0,1:T(8,128)S(1)}, u32[]{:S(2)}, u32[]{:S(2)}) %all-to-all-start) | async-done | bytes 655392 | tf_op jit(solution)/shard_map/all_to_all | solution.py:150
  35.4 131.3 %while.64 = (s32[]{:T(128)}, f32[10,16,1024]{2,0,1:T(8,128)}, s32[16]{0:T(128)S(1)}, f32[10,16,1024]{2,0,1:T(8,128)S(1)}, f32[4,1024,256]{2,1,0:T(8,128)}, /*ind...) while((s32[]{:T(128)}, f32[10,16,1024]{2,0,1:T(8,128)}, ...), condition=%wide.region_3.4_spmd.clone, body=%wide.region_0.3_spmd.clone.sunk | while | flops 62930964 | bytes 2478670 | solution.py:137
  36.6 4.6 while.65
  37.2 1.8 convolution_multiply_fusion.2
  39.1 2.2 convolution_add_fusion.2
  43.1 4.6 while.65
  43.7 1.8 convolution_multiply_fusion.2
  45.5 2.2 convolution_add_fusion.2
  49.6 4.6 while.65
  50.2 1.8 convolution_multiply_fusion.2
  52.0 2.2 convolution_add_fusion.2
  56.0 4.6 while.65
  56.6 1.8 convolution_multiply_fusion.2
  58.5 2.2 convolution_add_fusion.2
  62.5 4.6 while.65
  63.1 1.8 convolution_multiply_fusion.2
  64.9 2.2 convolution_add_fusion.2
  69.0 4.6 while.65
  71.4 2.2 convolution_add_fusion.2
  75.4 4.6 while.65
  77.9 2.2 convolution_add_fusion.2
  81.9 4.6 while.65
  84.3 2.2 convolution_add_fusion.2
  88.4 4.6 while.65
  90.8 2.2 convolution_add_fusion.2
  94.8 9.3 %while.65 = (s32[]{:T(128)}, f32[10,1024]{1,0:T(8,128)S(1)}, s32[]{:T(128)}, f32[4,1024,256]{2,1,0:T(8,128)}, f32[10,1024]{1,0:T(8,128)S(1)}, /*index=5*/s32[4,1...) while((s32[]{:T(128)}, f32[10,1024]{1,0:T(8,128)S(1)}, ...), condition=%wide.region_2.2_spmd, body=%wide.region_1.1_spmd.sunk | while | flops 62927876 | bytes 2244775 | solution.py:132
  95.4 1.8 convolution_multiply_fusion.2
  97.3 2.2 convolution_add_fusion.2
  101.9 2.2 convolution_add_fusion.2
  105.9 4.6 while.65
  108.4 2.2 convolution_add_fusion.2
  112.4 9.3 %while.65 = (s32[]{:T(128)}, f32[10,1024]{1,0:T(8,128)S(1)}, s32[]{:T(128)}, f32[4,1024,256]{2,1,0:T(8,128)}, f32[10,1024]{1,0:T(8,128)S(1)}, /*index=5*/s32[4,1...) while((s32[]{:T(128)}, f32[10,1024]{1,0:T(8,128)S(1)}, ...), condition=%wide.region_2.2_spmd, body=%wide.region_1.1_spmd.sunk | while | flops 62927876 | bytes 2244775 | solution.py:132
  114.8 2.2 convolution_add_fusion.2
  119.5 2.2 convolution_add_fusion.2
  123.5 9.3 %while.65 = (s32[]{:T(128)}, f32[10,1024]{1,0:T(8,128)S(1)}, s32[]{:T(128)}, f32[4,1024,256]{2,1,0:T(8,128)}, f32[10,1024]{1,0:T(8,128)S(1)}, /*index=5*/s32[4,1...) while((s32[]{:T(128)}, f32[10,1024]{1,0:T(8,128)S(1)}, ...), condition=%wide.region_2.2_spmd, body=%wide.region_1.1_spmd.sunk | while | flops 62927876 | bytes 2244775 | solution.py:132
  125.9 2.2 convolution_add_fusion.2
  130.6 2.2 convolution_add_fusion.2
  134.6 9.3 %while.65 = (s32[]{:T(128)}, f32[10,1024]{1,0:T(8,128)S(1)}, s32[]{:T(128)}, f32[4,1024,256]{2,1,0:T(8,128)}, f32[10,1024]{1,0:T(8,128)S(1)}, /*index=5*/s32[4,1...) while((s32[]{:T(128)}, f32[10,1024]{1,0:T(8,128)S(1)}, ...), condition=%wide.region_2.2_spmd, body=%wide.region_1.1_spmd.sunk | while | flops 62927876 | bytes 2244775 | solution.py:132
  137.1 2.2 convolution_add_fusion.2
  139.9 1.8 convolution_multiply_fusion.2
  141.7 2.2 convolution_add_fusion.2
  145.7 9.3 %while.65 = (s32[]{:T(128)}, f32[10,1024]{1,0:T(8,128)S(1)}, s32[]{:T(128)}, f32[4,1024,256]{2,1,0:T(8,128)}, f32[10,1024]{1,0:T(8,128)S(1)}, /*index=5*/s32[4,1...) while((s32[]{:T(128)}, f32[10,1024]{1,0:T(8,128)S(1)}, ...), condition=%wide.region_2.2_spmd, body=%wide.region_1.1_spmd.sunk | while | flops 62927876 | bytes 2244775 | solution.py:132
  146.3 1.8 convolution_multiply_fusion.2
  148.2 2.2 convolution_add_fusion.2
  152.8 2.2 convolution_add_fusion.2
  156.8 9.3 %while.65 = (s32[]{:T(128)}, f32[10,1024]{1,0:T(8,128)S(1)}, s32[]{:T(128)}, f32[4,1024,256]{2,1,0:T(8,128)}, f32[10,1024]{1,0:T(8,128)S(1)}, /*index=5*/s32[4,1...) while((s32[]{:T(128)}, f32[10,1024]{1,0:T(8,128)S(1)}, ...), condition=%wide.region_2.2_spmd, body=%wide.region_1.1_spmd.sunk | while | flops 62927876 | bytes 2244775 | solution.py:132
  159.3 2.2 convolution_add_fusion.2
  163.9 2.2 convolution_add_fusion.2
  166.7 7.1 %copy.31 = f32[10,16,1024]{0,1,2:T(8,128)} copy(f32[10,16,1024]{2,0,1:T(8,128)} %get-tuple-element.299) | data formatting | bytes 1310720 | tf_op jit(solution)/shard_map/while | solution.py:137
  173.9 9.5 %reshape.52 = f32[4,1,40960]{2,1,0:T(1,128)} reshape(f32[1024,16,10]{2,1,0:T(8,128)} %bitcast.58) | data formatting | bytes 1310720
  183.3 197.6 %all-to-all-start.1 = ((f32[4,1,40960]{2,1,0:T(1,128)}), f32[4,1,40960]{2,1,0:T(1,128)S(1)}, u32[]{:S(2)}, u32[]{:S(2)}) async-start(f32[4,1,40960]{2,1,0:T(1,128)} %reshape.52), calls=%async_computation.1 | async-start | bytes 1310720 | tf_op jit(solution)/shard_map/all_to_all | solution.py:157
  381.9 15.2 %all-to-all-done.1 = f32[4,1,40960]{2,1,0:T(1,128)S(1)} async-done(((f32[4,1,40960]{2,1,0:T(1,128)}), f32[4,1,40960]{2,1,0:T(1,128)S(1)}, u32[]{:S(2)}, u32[]{:S(2)}) %all-to-all-start.1) | async-done | bytes 655392 | tf_op jit(solution)/shard_map/all_to_all | solution.py:157
  397.6 2.5 reduce
  400.1 12.5 %reshape.53 = f32[1024,16,10]{2,1,0:T(8,128)} reshape(f32[4,40960]{1,0:T(4,128)S(1)} %reduce) | data formatting | bytes 1310720
  412.6 5.4 %copy.40 = f32[10,16,4,256]{3,2,1,0:T(4,128)S(1)} copy(f32[10,16,4,256]{0,1,3,2:T(8,128)} %bitcast.59) | data formatting | bytes 1310720 | tf_op jit(solution)/shard_map/all_to_all | solution.py:157
  420.6 4.7 collective-permute-done.2
  425.5 17.2 %collective-permute-done.1 = f32[5,2,256,96]{2,3,1,0:T(8,128)S(1)} collective-permute-done((f32[5,2,256,96]{2,3,1,0:T(8,128)}, f32[5,2,256,96]{2,3,1,0:T(8,128)S(1)}, u32[]{:S(2)}, u32[]{:S(2)}) %collective-permute-start.1) | collective-permute-done | bytes 983072 | tf_op jit(solution)/shard_map/ppermute | solution.py:29
  442.7 1.9 collective-permute-done
  445.5 2.5 fusion.49
  448.9 2.0 copy.35
  462.4 6.0 %fusion.11 = f32[5,6,260,100]{2,3,1,0:T(8,128)S(1)} fusion(f32[5,2,256,2]{2,3,1,0:T(2,128)S(1)} %broadcast_multiply_fusion.1, f32[5,6,260,2]{2,3,1,0:T(2,128)S(1)} %reshape.50, f32[5,6,2,96]{2,3,1,0:T(8,128)S(1)} %copy.37, f32[5,2,256,96]{2,3,1,0:T(8,128)S(1)} %copy-done.3, f32[5,2,256,32]{2,3,1,0:T(8,128)S(1)} %slice.186, ...), kind=kLoop, calls=%fused_computation.20 | loop fusion | flops 7020000 | bytes 6198080 | tf_op jit(solution)/shard_map/concatenate | solution.py:92
  (229 shorter events, 85.2 us)
Async XLA Ops:
  1.1 7.8 %copy-start.11 = (s32[64]{0:T(128)S(1)}, s32[64]{0:T(128)}, u32[]{:S(2)}) copy-start(s32[64]{0:T(128)} %param.10) | copy-start | bytes 772
  2.6 32.1 %all-to-all-start = ((f32[10,64,256]{2,0,1:T(8,128)}), f32[10,64,256]{2,0,1:T(8,128)S(1)}, u32[]{:S(2)}, u32[]{:S(2)}) async-start(f32[10,64,256]{2,0,1:T(8,128)} %copy.27), calls=%async_computation | async-start | bytes 2097152 | tf_op jit(solution)/shard_map/all_to_all | solution.py:150
  183.3 213.7 %all-to-all-start.1 = ((f32[4,1,40960]{2,1,0:T(1,128)}), f32[4,1,40960]{2,1,0:T(1,128)S(1)}, u32[]{:S(2)}, u32[]{:S(2)}) async-start(f32[4,1,40960]{2,1,0:T(1,128)} %reshape.52), calls=%async_computation.1 | async-start | bytes 1310720 | tf_op jit(solution)/shard_map/all_to_all | solution.py:157
  418.0 7.4 %copy-start.10 = (f32[5]{0:T(128)S(1)}, f32[5]{0:T(128)}, u32[]{:S(2)}) copy-start(f32[5]{0:T(128)} %constant.217.clone) | copy-start | bytes 64
  418.1 26.6 %copy-start = (f32[10,4,16,256]{3,2,1,0:T(8,128)}, f32[10,4,16,256]{3,2,1,0:T(8,128)S(1)}, u32[]{:S(2)}) copy-start(f32[10,4,16,256]{3,2,1,0:T(8,128)S(1)} %copy.33) | copy-start | bytes 1966084
  419.3 23.4 %collective-permute-start.1 = (f32[5,2,256,96]{2,3,1,0:T(8,128)}, f32[5,2,256,96]{2,3,1,0:T(8,128)S(1)}, u32[]{:S(2)}, u32[]{:S(2)}) collective-permute-start(f32[5,2,256,96]{2,3,1,0:T(8,128)} %pad_maximum_fusion.3), channel_id=1, source_target_pairs={{4,0},{8,4},{12,8},{16,12},{20,16},{24,20},{28,24},{0,28},{5,1},{9... | collective-permute-start | bytes 2949128 | tf_op jit(solution)/shard_map/ppermute | solution.py:29
  420.4 24.1 %collective-permute-start = (f32[5,2,256,96]{2,3,1,0:T(8,128)}, f32[5,2,256,96]{2,3,1,0:T(8,128)S(1)}, u32[]{:S(2)}, u32[]{:S(2)}) collective-permute-start(f32[5,2,256,96]{2,3,1,0:T(8,128)} %pad_maximum_fusion.3), channel_id=1, source_target_pairs={{0,4},{4,8},{8,12},{12,16},{16,20},{20,24},{24,28},{28,0},{1,5},{5... | collective-permute-start | bytes 2949128 | tf_op jit(solution)/shard_map/ppermute | solution.py:27
  420.5 4.7 collective-permute-start.2
  442.7 2.1 copy-start.2
  444.5 0.9 copy-start.4
  445.5 2.5 copy-start.6
  448.9 6.1 %copy-start.7 = (f32[5,6,256,96]{2,3,1,0:T(8,128)S(1)}, f32[5,6,256,96]{2,3,1,0:T(8,128)}, u32[]{:S(2)}) copy-start(f32[5,6,256,96]{2,3,1,0:T(8,128)} %copy-done.6) | copy-start | bytes 8847364
  450.8 8.0 %collective-permute-start.4 = (f32[5,6,2,96]{3,2,1,0:T(2,128)S(1)}, f32[5,6,2,96]{3,2,1,0:T(2,128)S(1)}, u32[]{:S(2)}, u32[]{:S(2)}) collective-permute-start(f32[5,6,2,96]{3,2,1,0:T(2,128)S(1)} %copy.35), channel_id=1, source_target_pairs={{1,0},{2,1},{3,2},{0,3},{5,4},{6,5},{7,6},{4,7},{9,8},{10,9},{11,1... | collective-permute-start | bytes 69128 | tf_op jit(solution)/shard_map/ppermute | solution.py:29
  454.2 5.9 %collective-permute-start.3 = (f32[5,6,2,96]{3,2,1,0:T(2,128)S(1)}, f32[5,6,2,96]{3,2,1,0:T(2,128)S(1)}, u32[]{:S(2)}, u32[]{:S(2)}) collective-permute-start(f32[5,6,2,96]{3,2,1,0:T(2,128)S(1)} %copy.34), channel_id=1, source_target_pairs={{0,1},{1,2},{2,3},{3,0},{4,5},{5,6},{6,7},{7,4},{8,9},{9,10},{10,1... | collective-permute-start | bytes 69128 | tf_op jit(solution)/shard_map/ppermute | solution.py:27
  460.6 1.4 copy-start.1
  460.6 1.5 copy-start.3
  460.6 1.8 copy-start.5
  470.2 1.8 copy-start.8
  473.0 1.2 copy-start.9
where the time goes:
time: 481 us; the launch traced here: 475 us
  starting transfers between devices  207 us (43%)
  matrix products  88.7 us (18%)
  local copies, waits for them, and re-layouts  70.8 us (15%)
  waiting for transfers between devices  54.9 us (11%)
  other arithmetic  42.2 us (9%)
  loops' own time  10.9 us (2%)
    all_to_all x1, starting transfers between devices, shards(): lax.all_to_all(smoothed, 'azim', split_axis=2, concat_axis=1, tiled=True)  198 us
    dot_general x22, matrix products, one_block(): lax.dot_general(scaled, basis_block, (((1,), (1,)), ((), ())), precision=...  48.3 us
    dot_general x22, matrix products, one_block(): coeffs = jnp.dot(cycle_values, basis_block, precision=lax.Precision.HIGHEST)  40.4 us
    unnamed x31, local copies, waits for them, and re-layouts  27.4 us
    ppermute x2, waiting for transfers between devices, with_halo(): lax.ppermute(head, axis, [((i + 1) % count, i) for i in range(count)])  17.2 us
    all_to_all x1, waiting for transfers between devices, shards(): lax.all_to_all(inner, 'azim', split_axis=1, concat_axis=2, tiled=True)  15.3 us
    all_to_all x1, waiting for transfers between devices, shards(): lax.all_to_all(smoothed, 'azim', split_axis=2, concat_axis=1, tiled=True)  15.2 us
    select_n x22, other arithmetic, one_block(): kept_weights = jnp.where(block_waves < mode_count, block_weights, 0.0)  12.2 us
  transfers between devices with their start and end apart: 7, of which 6 were waited for; matrix products, arithmetic and copies ran while one was open for 4% of the time, Pallas kernels for 0%

commit v1 on v0

--- a/solution.py
+++ b/solution.py
@@ -2,6 +2,7 @@
 
 import jax
 import jax.numpy as jnp
+import numpy as np
 from jax import lax
 from jax.sharding import PartitionSpec as P
 
@@ -92,49 +93,35 @@
     return jnp.concatenate([ghost, haloed, outer_cycles], axis=3)
 
 
-def fourier_tables():
+def fourier_basis():
     half_modes = NTH // 2
-    mode_block = min(128, half_modes)
-    block_count = half_modes // mode_block
-    wavenumbers = jnp.arange(half_modes, dtype=jnp.int32)
-    cell_numbers = jnp.arange(NTH, dtype=jnp.int32)
-    phase_index = cell_numbers[:, None] * wavenumbers[None, :] % NTH
-    angles = phase_index.astype(jnp.float32) * (2.0 * math.pi / NTH)
-    cosines = jnp.cos(angles).reshape(NTH, block_count, mode_block).transpose(1, 0, 2)
-    sines = jnp.sin(angles).reshape(NTH, block_count, mode_block).transpose(1, 0, 2)
-    tables = jnp.concatenate([cosines, sines], axis=2)
-    weights = (
-        jnp.where(wavenumbers == 0, 1.0 / NTH, 2.0 / NTH)
-        .astype(jnp.float32)
-        .reshape(block_count, mode_block)
-    )
-    return (tables, weights, wavenumbers.reshape(block_count, mode_block), mode_block)
+    block = 32
+    waves = np.arange(half_modes)
+    coarse = np.exp(2j * np.pi * (np.arange(0, NTH, block)[:, None] * waves % NTH) / NTH)
+    fine = np.exp(2j * np.pi * (np.arange(block)[:, None] * waves % NTH) / NTH)
+    coarse_cos = jnp.asarray(coarse.real, jnp.float32)[:, None]
+    coarse_sin = jnp.asarray(coarse.imag, jnp.float32)[:, None]
+    fine_cos = jnp.asarray(fine.real, jnp.float32)[None]
+    fine_sin = jnp.asarray(fine.imag, jnp.float32)[None]
+    cosines = (coarse_cos * fine_cos - coarse_sin * fine_sin).reshape(NTH, half_modes)
+    sines = (coarse_sin * fine_cos + coarse_cos * fine_sin).reshape(NTH, half_modes)
+    return jnp.concatenate([cosines, sines], axis=1)
 
 
-def truncate_cycles(slab, local_modes, tables, weights, wave_blocks, mode_block):
-
-    def one_cycle(cycle_index, result):
-        cycle_values = lax.dynamic_index_in_dim(slab, cycle_index, 1, keepdims=False)
-        mode_count = lax.dynamic_index_in_dim(local_modes, cycle_index, 0, keepdims=False)
-        used_blocks = (mode_count + mode_block - 1) // mode_block
-
-        def one_block(block_index, series_sum):
-            basis_block = lax.dynamic_index_in_dim(tables, block_index, 0, keepdims=False)
-            coeffs = jnp.dot(cycle_values, basis_block, precision=lax.Precision.HIGHEST)
-            block_waves = lax.dynamic_index_in_dim(wave_blocks, block_index, 0, keepdims=False)
-            block_weights = lax.dynamic_index_in_dim(weights, block_index, 0, keepdims=False)
-            kept_weights = jnp.where(block_waves < mode_count, block_weights, 0.0)
-            scaled = coeffs * jnp.concatenate([kept_weights, kept_weights])
-            return series_sum + lax.dot_general(
-                scaled, basis_block, (((1,), (1,)), ((), ())), precision=lax.Precision.HIGHEST
-            )
-
-        series = lax.fori_loop(
-            0, used_blocks, one_block, jnp.zeros(cycle_values.shape, jnp.float32)
-        )
-        return lax.dynamic_update_index_in_dim(result, series, cycle_index, 1)
-
-    return lax.fori_loop(0, slab.shape[1], one_cycle, jnp.zeros(slab.shape, jnp.float32))
+def truncate_cycles(slab, local_modes):
+    items, cycles, cells = slab.shape
+    half_modes = NTH // 2
+    basis = fourier_basis()
+    rows = slab.reshape(items * cycles, cells)
+    coeffs = jnp.dot(rows, basis, precision=lax.Precision.HIGH)
+    wave = jnp.arange(2 * half_modes, dtype=jnp.int32) % half_modes
+    weight = jnp.where(wave == 0, 1.0 / NTH, 2.0 / NTH).astype(jnp.float32)
+    kept = jnp.where(wave[None, :] < local_modes[:, None], weight[None, :], 0.0)
+    coeffs = (coeffs.reshape(items, cycles, 2 * half_modes) * kept[None]).reshape(items * cycles, -1)
+    series = lax.dot_general(
+        coeffs, basis, (((1,), (1,)), ((), ())), precision=lax.Precision.HIGH
+    )
+    return series.reshape(items, cycles, cells)
 
 
 def shards(state, start, modes):
@@ -143,16 +130,11 @@
     azim_index = lax.axis_index("azim")
     cycles_local = NIN // azim_size
     item_count = field_count * axial_local
-    tables, weights, wave_blocks, mode_block = fourier_tables()
     inner = state[..., :NIN].transpose(0, 1, 3, 2).reshape(item_count, NIN, theta_local)
     local_modes = lax.dynamic_slice_in_dim(modes, azim_index * cycles_local, cycles_local)
     smoothed = truncate_cycles(
         lax.all_to_all(inner, "azim", split_axis=1, concat_axis=2, tiled=True),
         local_modes,
-        tables,
-        weights,
-        wave_blocks,
-        mode_block,
     )
     exchanged = lax.all_to_all(smoothed, "azim", split_axis=2, concat_axis=1, tiled=True)
     smooth_inner = exchanged.reshape(field_count, axial_local, NIN, theta_local).transpose(

time: 481 us -> 145 us (0.30); the launches traced: 475 us -> 144 us
  starting transfers between devices: 207 us -> 13.5 us
  matrix products: 88.7 us -> 3.72 us
  local copies, waits for them, and re-layouts: 70.8 us -> 41.6 us
  other arithmetic: 42.2 us -> 21.3 us
  loops' own time: 10.9 us -> 0 us
  waiting for transfers between devices: 54.9 us -> 63.5 us
    all_to_all x1, starting transfers between devices: 198 us -> 3.66 us  [shards(): lax.all_to_all(smoothed, 'azim', split_axis=2, concat_axis=1, tiled=True)]
    dot_general x44 -> x2, matrix products: 88.7 us -> 3.72 us  [the longest x1 2.35 us: truncate_cycles(): lax.dot_general(coeffs, basis, (((1,), (1,)), ((), ())), precision=lax.Pr...]
    select_n x38 -> x3, other arithmetic: 12.3 us -> 0.08 us  [the longest x1 0.08 us: truncate_cycles(): kept = jnp.where(wave[None, :] < local_modes[:, None], weight[None, :], 0.0)]
    another operation x17 -> x0, loops' own time: 10.9 us -> none  [the longest x1 9.76 us: truncate_cycles(): lax.fori_loop(0, slab.shape[1], one_cycle, jnp.zeros(slab.shape, jnp.floa...]
    dynamic_update_slice x16 -> x0, local copies, waits for them, and re-layouts: 10 us -> none  [one_cycle(): return lax.dynamic_update_index_in_dim(result, series, cycle_index, 1)]
    unnamed x31 -> x40, local copies, waits for them, and re-layouts: 27.4 us -> 17.9 us
    dynamic_slice x16 -> x0, local copies, waits for them, and re-layouts: 8.84 us -> none  [one_cycle(): lax.dynamic_index_in_dim(local_modes, cycle_index, 0, keepdims=False)]
    all_to_all x1, waiting for transfers between devices: 15.3 us -> 23.5 us  [shards(): lax.all_to_all(inner, 'azim', split_axis=1, concat_axis=2, tiled=True)]
  transfers between devices with their start and end apart: 7 -> 7, of which waited for: 6 -> 6; matrix products, arithmetic and copies ran while one was open for 4% -> 7% of each run, Pallas kernels for 0% -> 0%
where the time goes in v1:
time: 145 us; the launch traced here: 144 us
  waiting for transfers between devices  63.5 us (44%)
  local copies, waits for them, and re-layouts  41.6 us (29%)
  other arithmetic  21.3 us (15%)
  starting transfers between devices  13.5 us (9%)
  matrix products  3.72 us (3%)
    all_to_all x1, waiting for transfers between devices, shards(): lax.all_to_all(inner, 'azim', split_axis=1, concat_axis=2, tiled=True)  23.5 us
    unnamed x40, local copies, waits for them, and re-layouts  17.9 us
    ppermute x2, waiting for transfers between devices, with_halo(): lax.ppermute(head, axis, [((i + 1) % count, i) for i in range(count)])  17.2 us
    all_to_all x1, waiting for transfers between devices, shards(): lax.all_to_all(smoothed, 'azim', split_axis=2, concat_axis=1, tiled=True)  15.6 us
    all_to_all x1, starting transfers between devices, shards(): lax.all_to_all(inner, 'azim', split_axis=1, concat_axis=2, tiled=True)  6.35 us
    dot_general x1, local copies, waits for them, and re-layouts, truncate_cycles(): lax.dot_general(coeffs, basis, (((1,), (1,)), ((), ())), precision=lax.Pr...  6.18 us
    all_to_all x3, local copies, waits for them, and re-layouts, shards(): lax.all_to_all(smoothed, 'azim', split_axis=2, concat_axis=1, tiled=True)  6.09 us
    concatenate x1, other arithmetic, radial_extend(): return jnp.concatenate([ghost, haloed, outer_cycles], axis=3)  6.04 us
  transfers between devices with their start and end apart: 7, of which 6 were waited for; matrix products, arithmetic and copies ran while one was open for 7% of the time, Pallas kernels for 0%

profile of v1, /device:TPU:0, one launch (start us, length us, event | category | flops | bytes accessed | tf_op | source)
XLA Modules:
  0.0 144.2 jit_solution(8314148820570788097)
XLA Ops:
  0.0 1.1 slice.185
  1.2 1.4 copy.24
  2.6 6.3 %all-to-all-start = ((f32[10,64,256]{2,0,1:T(8,128)}), f32[10,64,256]{2,0,1:T(8,128)S(1)}, u32[]{:S(2)}, u32[]{:S(2)}) async-start(f32[10,64,256]{2,0,1:T(8,128)} %copy.24), calls=%async_computation | async-start | bytes 2097152 | tf_op jit(solution)/shard_map/all_to_all | solution.py:136
  9.0 0.1 compare_select_fusion
  9.1 2.0 %multiply_subtract_fusion = (f32[32,32,512]{2,1,0:T(8,128)S(1)}, f32[32,32,512]{2,1,0:T(8,128)}) fusion(f32[32,512]{1,0:T(8,128)S(1)} %copy-done.11, f32[32,512]{1,0:T(8,128)S(1)} %copy-done.12, f32[32,512]{1,0:T(8,128)S(1)} %copy-done.13, f32[32,512]{1,0:T(8,128)S(1)} %copy-done.14), kind=kLoop, calls=%fused_computation.15 | loop fusion | flops 3145728 | bytes 4456448 | tf_op jit(solution)/shard_map/sub | solution.py:106
  11.1 23.5 %all-to-all-done = f32[10,64,256]{2,0,1:T(8,128)S(1)} async-done(((f32[10,64,256]{2,0,1:T(8,128)}), f32[10,64,256]{2,0,1:T(8,128)S(1)}, u32[]{:S(2)}, u32[]{:S(2)}) %all-to-all-start) | async-done | bytes 655392 | tf_op jit(solution)/shard_map/all_to_all | solution.py:136
  34.7 0.4 copy.26
  35.1 0.1 copy.37
  35.3 1.0 copy-done.8
  36.3 1.4 fusion.5
  37.6 2.3 %fusion.1 = f32[10,16,1024]{2,1,0:T(8,128)S(1)} fusion(f32[10,16,1024]{2,1,0:T(8,128)S(1)} %bitcast.54, f32[1024,512]{1,0:T(8,128)S(1)} %bitcast.47, f32[1024,512]{1,0:T(8,128)S(1)} %bitcast.45), kind=kOutput, calls=%fused_computation.4 | convolution fusion | flops 1007681536 | bytes 5505024 | tf_op jit(solution)/shard_map/dot_general | solution.py:121
  40.0 6.2 %copy.27 = f32[10,16,1024]{1,0,2:T(8,128)} copy(f32[10,16,1024]{2,1,0:T(8,128)S(1)} %fusion.1) | data formatting | bytes 1310720 | tf_op jit(solution)/shard_map/dot_general | solution.py:121
  46.2 5.8 %reshape.108 = f32[4,1,40960]{2,1,0:T(1,128)} reshape(f32[1024,10,16]{2,1,0:T(8,128)} %bitcast.42) | data formatting | bytes 1310720
  52.0 3.7 %all-to-all-start.1 = ((f32[4,1,40960]{2,1,0:T(1,128)}), f32[4,1,40960]{2,1,0:T(1,128)S(1)}, u32[]{:S(2)}, u32[]{:S(2)}) async-start(f32[4,1,40960]{2,1,0:T(1,128)} %reshape.108), calls=%async_computation.1 | async-start | bytes 1310720 | tf_op jit(solution)/shard_map/all_to_all | solution.py:139
  55.7 1.0 slice.186
  56.7 15.6 %all-to-all-done.1 = f32[4,1,40960]{2,1,0:T(1,128)S(1)} async-done(((f32[4,1,40960]{2,1,0:T(1,128)}), f32[4,1,40960]{2,1,0:T(1,128)S(1)}, u32[]{:S(2)}, u32[]{:S(2)}) %all-to-all-start.1) | async-done | bytes 655392 | tf_op jit(solution)/shard_map/all_to_all | solution.py:139
  72.3 0.5 broadcast.159
  72.9 2.5 %reduce = f32[4,40960]{1,0:T(4,128)S(1)} reduce(f32[4,1,40960]{2,1,0:T(1,128)S(1)} %all-to-all-done.1, f32[]{:T(128)} %broadcast.159), dimensions={1}, to_apply=%all_to_all.25.reduce_sub_computation | reduce | bytes 1310724 | tf_op jit(solution)/shard_map/all_to_all | solution.py:139
  75.4 6.2 %reshape.109 = f32[1024,10,16]{2,1,0:T(8,128)} reshape(f32[4,40960]{1,0:T(4,128)S(1)} %reduce) | data formatting | bytes 1310720
  81.6 5.5 %copy.35 = f32[10,16,4,256]{3,2,1,0:T(4,128)S(1)} copy(f32[10,16,4,256]{1,0,3,2:T(8,128)} %bitcast.43) | data formatting | bytes 1310720 | tf_op jit(solution)/shard_map/all_to_all | solution.py:139
  87.1 0.1 copy.29
  87.2 1.1 pad_maximum_fusion.4
  88.4 1.2 collective-permute-start.1
  89.5 0.1 broadcast_multiply_fusion.3
  89.7 4.7 %collective-permute-done.2 = f32[5,2,256,2]{2,3,1,0:T(2,128)S(1)} collective-permute-done((f32[5,2,256,2]{2,3,1,0:T(2,128)S(1)}, f32[5,2,256,2]{2,3,1,0:T(2,128)S(1)}, u32[]{:S(2)}, u32[]{:S(2)}) %collective-permute-start.2) | collective-permute-done | bytes 20512 | tf_op jit(solution)/shard_map/ppermute | solution.py:18
  94.3 0.1 rev.4
  94.5 0.1 broadcast_multiply_fusion.1
  94.5 17.2 %collective-permute-done.1 = f32[5,2,256,96]{2,3,1,0:T(8,128)S(1)} collective-permute-done((f32[5,2,256,96]{2,3,1,0:T(8,128)}, f32[5,2,256,96]{2,3,1,0:T(8,128)S(1)}, u32[]{:S(2)}, u32[]{:S(2)}) %collective-permute-start.1) | collective-permute-done | bytes 983072 | tf_op jit(solution)/shard_map/ppermute | solution.py:30
  111.7 1.9 %collective-permute-done = f32[5,2,256,96]{2,3,1,0:T(8,128)S(1)} collective-permute-done((f32[5,2,256,96]{2,3,1,0:T(8,128)}, f32[5,2,256,96]{2,3,1,0:T(8,128)S(1)}, u32[]{:S(2)}, u32[]{:S(2)}) %collective-permute-start) | collective-permute-done | bytes 983072 | tf_op jit(solution)/shard_map/ppermute | solution.py:28
  113.6 0.2 pad_maximum_fusion.3
  113.8 0.7 copy-done.4
  114.6 2.5 %fusion.40 = (f32[5,6,2,96]{2,3,1,0:T(8,128)}, f32[5,6,2,96]{2,3,1,0:T(8,128)}) fusion(f32[5,6,256,96]{2,3,1,0:T(8,128)S(1)} %pad_maximum_fusion.3), kind=kLoop, calls=%fused_computation.108 | loop fusion | bytes 92160 | tf_op jit(solution)/shard_map/slice | solution.py:25
  117.1 0.9 slice_dynamic-update-slice_fusion
  117.9 2.0 %copy.31 = f32[5,6,2,96]{3,2,1,0:T(2,128)S(1)} copy(f32[5,6,2,96]{2,3,1,0:T(8,128)} %get-tuple-element.24) | data formatting | bytes 46080 | tf_op jit(solution)/shard_map/slice | solution.py:24
  119.9 1.3 collective-permute-start.4
  121.2 1.8 %copy.30 = f32[5,6,2,96]{3,2,1,0:T(2,128)S(1)} copy(f32[5,6,2,96]{2,3,1,0:T(8,128)} %get-tuple-element.23) | data formatting | bytes 46080 | tf_op jit(solution)/shard_map/slice | solution.py:25
  123.1 1.0 collective-permute-start.3
  124.0 1.1 add_dynamic-update-slice_fusion
  125.1 0.9 multiply_dynamic-update-slice_fusion.2
  126.0 0.9 multiply_dynamic-update-slice_fusion.1
  127.0 0.9 multiply_dynamic-update-slice_fusion
  127.9 0.5 copy.33
  128.4 0.6 collective-permute-done.3
  129.0 0.5 copy.32
  129.5 1.3 pad_maximum_fusion.17
  130.9 0.1 copy-done.3
  131.0 0.3 copy-done.5
  131.3 6.0 %fusion = f32[5,6,260,100]{2,3,1,0:T(8,128)S(1)} fusion(f32[5,2,256,2]{2,3,1,0:T(2,128)S(1)} %broadcast_multiply_fusion.1, f32[5,6,260,2]{2,3,1,0:T(2,128)S(1)} %reshape.106, f32[5,6,2,96]{2,3,1,0:T(8,128)S(1)} %copy.33, f32[5,2,256,96]{2,3,1,0:T(8,128)S(1)} %copy-done.3, f32[5,2,256,32]{2,3,1,0:T(8,128)S(1)} %slice.186, f32[5,2,256,64]{2,3,1,0:T(8,128)S(1)} %bitcast.36, ...), kind=kLoop, calls=%fused_computation.1 | loop fusion | flops 7020000 | bytes 6198080 | tf_op jit(solution)/shard_map/concatenate | solution.py:93
  137.3 0.1 slice_dynamic-update-slice_fusion.1
  137.5 0.2 multiply_dynamic-update-slice_fusion.8
  137.7 0.3 add_dynamic-update-slice_fusion.2
  138.1 0.1 multiply_dynamic-update-slice_fusion.7
  138.2 0.1 multiply_dynamic-update-slice_fusion.6
  138.3 0.1 broadcast_multiply_fusion
  138.5 0.2 constant_dynamic-update-slice_fusion
  138.6 0.3 multiply_dynamic-update-slice_fusion.5
  138.9 0.2 multiply_dynamic-update-slice_fusion.4
  139.1 0.2 add_dynamic-update-slice_fusion.1
  139.3 0.1 multiply_dynamic-update-slice_fusion.3
  139.4 1.5 %copy-done.9 = f32[5,6,256,96]{2,3,1,0:T(8,128)S(1)} copy-done((f32[5,6,256,96]{2,3,1,0:T(8,128)S(1)}, f32[5,6,256,96]{2,3,1,0:T(8,128)}, u32[]{:S(2)}) %copy-start.9) | copy-done | bytes 2949144
  140.9 0.9 fusion.9
  141.9 0.1 fusion.27
  142.1 1.0 copy-done.10
  143.1 1.1 fusion.18
  (41 shorter events, 0.4 us)
Async XLA Ops:
  1.1 7.8 %copy-start.16 = (s32[64]{0:T(128)S(1)}, s32[64]{0:T(128)}, u32[]{:S(2)}) copy-start(s32[64]{0:T(128)} %param.10) | copy-start | bytes 772
  1.2 8.0 %copy-start.11 = (f32[32,512]{1,0:T(8,128)S(1)}, f32[32,512]{1,0:T(8,128)}, u32[]{:S(2)}) copy-start(f32[32,512]{1,0:T(8,128)} %constant.78.clone) | copy-start | bytes 196612
  1.2 8.0 %copy-start.12 = (f32[32,512]{1,0:T(8,128)S(1)}, f32[32,512]{1,0:T(8,128)}, u32[]{:S(2)}) copy-start(f32[32,512]{1,0:T(8,128)} %constant.76.clone) | copy-start | bytes 196612
  1.2 7.9 %copy-start.13 = (f32[32,512]{1,0:T(8,128)S(1)}, f32[32,512]{1,0:T(8,128)}, u32[]{:S(2)}) copy-start(f32[32,512]{1,0:T(8,128)} %constant.77.clone) | copy-start | bytes 196612
  1.2 7.9 %copy-start.14 = (f32[32,512]{1,0:T(8,128)S(1)}, f32[32,512]{1,0:T(8,128)}, u32[]{:S(2)}) copy-start(f32[32,512]{1,0:T(8,128)} %constant.75.clone) | copy-start | bytes 196612
  2.6 32.1 %all-to-all-start = ((f32[10,64,256]{2,0,1:T(8,128)}), f32[10,64,256]{2,0,1:T(8,128)S(1)}, u32[]{:S(2)}, u32[]{:S(2)}) async-start(f32[10,64,256]{2,0,1:T(8,128)} %copy.24), calls=%async_computation | async-start | bytes 2097152 | tf_op jit(solution)/shard_map/all_to_all | solution.py:136
  34.7 1.6 %copy-start.8 = (f32[32,32,512]{2,1,0:T(8,128)S(1)}, f32[32,32,512]{2,1,0:T(8,128)}, u32[]{:S(2)}) copy-start(f32[32,32,512]{2,1,0:T(8,128)} %get-tuple-element.29) | copy-start | bytes 6291460
  52.0 20.3 %all-to-all-start.1 = ((f32[4,1,40960]{2,1,0:T(1,128)}), f32[4,1,40960]{2,1,0:T(1,128)S(1)}, u32[]{:S(2)}, u32[]{:S(2)}) async-start(f32[4,1,40960]{2,1,0:T(1,128)} %reshape.108), calls=%async_computation.1 | async-start | bytes 1310720 | tf_op jit(solution)/shard_map/all_to_all | solution.py:139
  87.1 7.4 %copy-start.15 = (f32[5]{0:T(128)S(1)}, f32[5]{0:T(128)}, u32[]{:S(2)}) copy-start(f32[5]{0:T(128)} %constant.79.clone) | copy-start | bytes 64
  87.2 26.6 %copy-start = (f32[10,4,16,256]{3,2,1,0:T(8,128)}, f32[10,4,16,256]{3,2,1,0:T(8,128)S(1)}, u32[]{:S(2)}) copy-start(f32[10,4,16,256]{3,2,1,0:T(8,128)S(1)} %copy.29) | copy-start | bytes 1966084
  88.4 23.4 %collective-permute-start.1 = (f32[5,2,256,96]{2,3,1,0:T(8,128)}, f32[5,2,256,96]{2,3,1,0:T(8,128)S(1)}, u32[]{:S(2)}, u32[]{:S(2)}) collective-permute-start(f32[5,2,256,96]{2,3,1,0:T(8,128)} %pad_maximum_fusion.4), channel_id=1, source_target_pairs={{4,0},{8,4},{12,8},{16,12},{20,16},{24,20},{28,24},{0,28},{5,1},{9... | collective-permute-start | bytes 2949128 | tf_op jit(solution)/shard_map/ppermute | solution.py:30
  89.5 24.1 %collective-permute-start = (f32[5,2,256,96]{2,3,1,0:T(8,128)}, f32[5,2,256,96]{2,3,1,0:T(8,128)S(1)}, u32[]{:S(2)}, u32[]{:S(2)}) collective-permute-start(f32[5,2,256,96]{2,3,1,0:T(8,128)} %pad_maximum_fusion.4), channel_id=1, source_target_pairs={{0,4},{4,8},{8,12},{12,16},{16,20},{20,24},{24,28},{28,0},{1,5},{5... | collective-permute-start | bytes 2949128 | tf_op jit(solution)/shard_map/ppermute | solution.py:28
  89.6 4.7 %collective-permute-start.2 = (f32[5,2,256,2]{2,3,1,0:T(2,128)S(1)}, f32[5,2,256,2]{2,3,1,0:T(2,128)S(1)}, u32[]{:S(2)}, u32[]{:S(2)}) collective-permute-start(f32[5,2,256,2]{2,3,1,0:T(2,128)S(1)} %slice.238), channel_id=1, source_target_pairs={{0,2},{1,3},{2,0},{3,1},{4,6},{5,7},{6,4},{7,5},{8,10},{9,11},{10,... | collective-permute-start | bytes 61448 | tf_op jit(solution)/shard_map/ppermute | solution.py:18
  111.7 2.1 %copy-start.2 = (f32[5,2,256,96]{2,3,1,0:T(8,128)}, f32[5,2,256,96]{2,3,1,0:T(8,128)S(1)}, u32[]{:S(2)}) copy-start(f32[5,2,256,96]{2,3,1,0:T(8,128)S(1)} %collective-permute-done.1) | copy-start | bytes 2949124
  113.6 0.9 copy-start.4
  114.6 2.5 %copy-start.6 = (f32[5,6,256,96]{2,3,1,0:T(8,128)}, f32[5,6,256,96]{2,3,1,0:T(8,128)S(1)}, u32[]{:S(2)}) copy-start(f32[5,6,256,96]{2,3,1,0:T(8,128)S(1)} %pad_maximum_fusion.3) | copy-start | bytes 8847364
  117.9 6.1 %copy-start.7 = (f32[5,6,256,96]{2,3,1,0:T(8,128)S(1)}, f32[5,6,256,96]{2,3,1,0:T(8,128)}, u32[]{:S(2)}) copy-start(f32[5,6,256,96]{2,3,1,0:T(8,128)} %copy-done.6) | copy-start | bytes 8847364
  119.9 8.0 %collective-permute-start.4 = (f32[5,6,2,96]{3,2,1,0:T(2,128)S(1)}, f32[5,6,2,96]{3,2,1,0:T(2,128)S(1)}, u32[]{:S(2)}, u32[]{:S(2)}) collective-permute-start(f32[5,6,2,96]{3,2,1,0:T(2,128)S(1)} %copy.31), channel_id=1, source_target_pairs={{1,0},{2,1},{3,2},{0,3},{5,4},{6,5},{7,6},{4,7},{9,8},{10,9},{11,1... | collective-permute-start | bytes 69128 | tf_op jit(solution)/shard_map/ppermute | solution.py:30
  123.1 5.9 %collective-permute-start.3 = (f32[5,6,2,96]{3,2,1,0:T(2,128)S(1)}, f32[5,6,2,96]{3,2,1,0:T(2,128)S(1)}, u32[]{:S(2)}, u32[]{:S(2)}) collective-permute-start(f32[5,6,2,96]{3,2,1,0:T(2,128)S(1)} %copy.30), channel_id=1, source_target_pairs={{0,1},{1,2},{2,3},{3,0},{4,5},{5,6},{6,7},{7,4},{8,9},{9,10},{10,1... | collective-permute-start | bytes 69128 | tf_op jit(solution)/shard_map/ppermute | solution.py:28
  129.5 1.4 copy-start.1
  129.5 1.5 %copy-start.3 = (f32[5,2,256,96]{2,3,1,0:T(8,128)S(1)}, f32[5,2,256,96]{2,3,1,0:T(8,128)}, u32[]{:S(2)}) copy-start(f32[5,2,256,96]{2,3,1,0:T(8,128)} %copy-done.2) | copy-start | bytes 2949124
  129.5 1.8 %copy-start.5 = (f32[5,2,256,96]{2,3,1,0:T(8,128)S(1)}, f32[5,2,256,96]{2,3,1,0:T(8,128)}, u32[]{:S(2)}) copy-start(f32[5,2,256,96]{2,3,1,0:T(8,128)} %copy-done.4) | copy-start | bytes 2949124
  139.1 1.8 %copy-start.9 = (f32[5,6,256,96]{2,3,1,0:T(8,128)S(1)}, f32[5,6,256,96]{2,3,1,0:T(8,128)}, u32[]{:S(2)}) copy-start(f32[5,6,256,96]{2,3,1,0:T(8,128)} %multiply_dynamic-update-slice_fusion) | copy-start | bytes 8847364
  141.9 1.2 copy-start.10

commit v2 on v1

v2 whole, which is shorter than its diff:
```python
import functools
import math

import jax
import jax.numpy as jnp
import numpy as np
from jax import lax
from jax.experimental import pallas as pl
from jax.experimental.pallas import tpu as pltpu
from jax.sharding import PartitionSpec as P

NTH = 1024
NIN = 64
MSTEP = 8
STEP_DT = 0.05
LANES = 128
RIM = 8
F32 = jnp.float32
BF16 = jnp.bfloat16
MESH = pl.DeviceIdType.MESH


def split_np(values):
    high = values.astype(np.float32).astype(jnp.bfloat16)
    low = (values - high.astype(np.float64)).astype(np.float32).astype(jnp.bfloat16)
    return np.stack([high, low])


@functools.lru_cache(None)
def plan(cells):
    order = np.arange(1, NIN + 1)
    kept = np.minimum(2 * MSTEP * order, NTH // 2)
    dropped = NTH // 2 + 1 - np.minimum(MSTEP * order, NTH // 2)
    use_kept = kept <= dropped
    bound = np.where(use_kept, kept, dropped)
    first_dropped = int(np.argmin(use_kept))
    ranked = np.argsort(-bound, kind="stable")
    pairs = NIN // 2
    top, bottom = ranked[:pairs], ranked[::-1][:pairs]
    rows = int(-(-np.max(bound[top] + bound[bottom]) // 16) * 16)
    wave = np.arange(rows)
    angle = lambda n, q: 2 * np.pi * ((n * q) % NTH) / NTH
    forward = []
    for waves in (wave, wave[::-1]):
        phase = angle(np.arange(cells)[None, :], waves[:, None])
        forward.append(split_np(np.concatenate([np.cos(phase), np.sin(phase)], 0)))
    inverse = []
    for waves in (wave, wave[::-1]):
        phase = angle(np.arange(-RIM, cells + RIM)[:, None], waves[None, :])
        inverse.append(split_np(np.concatenate([np.cos(phase), np.sin(phase)], 1)))
    slots = LANES // pairs
    place = np.zeros((slots + slots // 2, LANES, 2 * LANES), np.float32)
    ghost = np.zeros((slots + slots // 2, LANES, LANES), np.float32)
    for slot in range(slots):
        for pair in range(pairs):
            place[slot, top[pair], slot * pairs + pair] = 1
            place[slot, bottom[pair], LANES + slot * pairs + pair] = 1
            if bottom[pair] < 2:
                ghost[slot, slot * pairs + pair, LANES - 1 - bottom[pair]] = 1
    half = slots // 2
    for k in range(half):
        place[slots + k] = place[k] + place[half + k]
        ghost[slots + k] = ghost[k] + ghost[half + k]
    top_rows = np.tile(bound[top], slots)
    wave_of = np.where(wave[:, None] < top_rows[None, :], wave[:, None], rows - 1 - wave[:, None])
    turn = angle(cells, wave_of)
    return dict(
        rows=rows,
        top=top,
        bottom=bottom,
        slots=slots,
        first_dropped=first_dropped,
        top_rows=top_rows.astype(np.int32),
        forward=np.stack(forward),
        inverse=np.stack(inverse),
        place=place.astype(jnp.bfloat16),
        back=place.transpose(0, 2, 1).astype(jnp.bfloat16),
        ghost=ghost.astype(jnp.bfloat16),
        turn=np.stack([np.cos(turn), np.sin(turn)]).astype(np.float32),
    )


def split(values):
    high = values.astype(BF16)
    return high, (values - high.astype(F32)).astype(BF16)


def mm(a, b):
    return jnp.dot(a, b, preferred_element_type=F32)


def fluxes(values, direction):
    inverse = 1.0 / values[0]
    velocity = values[direction] * inverse
    kinetic = (values[1] * values[1] + values[2] * values[2] + values[3] * values[3]) * inverse
    pressure = 0.4 * (values[4] - 0.5 * kinetic)
    parts = [
        values[direction],
        values[1] * velocity,
        values[2] * velocity,
        values[3] * velocity,
        (values[4] + pressure) * velocity,
    ]
    parts[direction] = parts[direction] + pressure
    return parts, inverse, pressure


def kernel(
    cfg,
    state, limits, forward, inverse, place, back, ghost, turn,
    out,
    ext, outer_own, outer_left, outer_right, inner_own, inner_left, inner_right,
    own, to_right, to_left, from_left, from_right, spectrum,
    halo_send, halo_recv, outer_send, outer_recv, inner_send, inner_recv, wave_send, wave_recv,
):
    rows, first_dropped = cfg["rows"], cfg["first_dropped"]
    half = rows // 2
    fields, cells, cycles = state.shape[0], state.shape[2], out.shape[3]
    tall = cells + 2 * RIM
    d, count = lax.axis_index("azim"), lax.axis_size("azim")
    a, ring = lax.axis_index("axial"), lax.axis_size("axial")
    z_right = {"azim": lax.rem(d + 1, count)}
    z_left = {"azim": lax.rem(d + count - 1, count)}
    x_right = {"axial": lax.rem(a + 1, ring)}
    x_left = {"axial": lax.rem(a + ring - 1, ring)}

    def remote(src, dst, send, recv, device):
        return pltpu.make_async_remote_copy(
            src_ref=src, dst_ref=dst, send_sem=send, recv_sem=recv,
            device_id=device, device_id_type=MESH,
        )

    barrier = pltpu.get_barrier_semaphore()
    for device in (z_right, z_left, x_right, x_left):
        pl.semaphore_signal(barrier, inc=1, device_id=device, device_id_type=MESH)
    pl.semaphore_wait(barrier, 4)

    halos = [
        remote(
            state.at[:, :, pl.ds(cells - RIM, RIM)], ext.at[:, :, pl.ds(0, RIM)],
            halo_send.at[0], halo_recv.at[0], z_right,
        ),
        remote(
            state.at[:, :, pl.ds(0, RIM)], ext.at[:, :, pl.ds(cells + RIM, RIM)],
            halo_send.at[1], halo_recv.at[1], z_left,
        ),
    ]
    outers = [
        remote(outer_own, outer_left, outer_send.at[0], outer_recv.at[0], x_right),
        remote(outer_own, outer_right, outer_send.at[1], outer_recv.at[1], x_left),
    ]
    chunks = 5
    rights = [
        remote(to_right.at[c], from_left.at[c], wave_send.at[0, c], wave_recv.at[0, c], z_right)
        for c in range(chunks)
    ]
    lefts = [
        remote(to_left.at[c], from_right.at[c], wave_send.at[1, c], wave_recv.at[1, c], z_left)
        for c in range(chunks)
    ]
    inners = [
        [
            remote(inner_own.at[f], inner_left.at[f], inner_send.at[0, f], inner_recv.at[0, f], x_right),
            remote(inner_own.at[f], inner_right.at[f], inner_send.at[1, f], inner_recv.at[1, f], x_left),
        ]
        for f in range(fields)
    ]
    is_first, is_last = d == 0, d == count - 1

    lane_cells = lax.broadcasted_iota(jnp.int32, (cells, LANES), 1)
    parity_cells = (1 - 2 * (lax.broadcasted_iota(jnp.int32, (cells, LANES), 0) & 1)).astype(F32)
    signs = jnp.where(lane_cells >= first_dropped, parity_cells, 1.0)
    row_ids = lax.broadcasted_iota(jnp.int32, (half, LANES), 0)
    low_lanes = lax.broadcasted_iota(jnp.int32, (half, LANES), 1) < LANES // 2
    top_keep = limits[0:1, :]
    bottom_keep = limits[1:2, :]
    top_rows = limits[2:3, :]

    def tile_items(tile):
        if tile < 2:
            return [(4 * tile + k, k) for k in range(4)]
        return [(8, 4), (9, 5)]

    def tile_chunks(tile):
        return [2 * tile, 2 * tile + 1] if tile < 2 else [4]

    for tile in range(3):
        high = jnp.zeros((cells, 2 * LANES), F32)
        low = jnp.zeros((cells, 2 * LANES), F32)
        for item, slot in tile_items(tile):
            item_high, item_low = split(state[item // 2, item % 2] * signs)
            high = high + mm(item_high, place[slot])
            low = low + mm(item_low, place[slot])
        high, low = high.astype(BF16), low.astype(BF16)
        for part in range(2):
            pieces = []
            for side in range(2):
                window = pl.ds(part * rows + side * half, half)
                sums = []
                for which in range(2):
                    lanes = slice(which * LANES, (which + 1) * LANES)
                    table_high, table_low = forward[which, 0, window, :], forward[which, 1, window, :]
                    sums.append(
                        mm(table_high, high[:, lanes])
                        + mm(table_high, low[:, lanes])
                        + mm(table_low, high[:, lanes])
                    )
                pieces.append(jnp.where(row_ids + side * half < top_rows, sums[0], sums[1]))
            if tile < 2:
                own[2 * tile, part] = pieces[0]
                own[2 * tile + 1, part] = pieces[1]
            else:
                own[4, part] = jnp.where(low_lanes, pieces[0], pieces[1])
        for c in tile_chunks(tile):
            @pl.when(is_first)
            def _():
                to_right[c] = own[c]
                rights[c].start()

            @pl.when(is_last)
            def _():
                to_left[c] = own[c]
                lefts[c].start()
        if tile == 0:
            for copy in halos:
                copy.start()

    for f in range(fields):
        outer_own[f] = jnp.where(
            lane_cells < LANES // 2, pltpu.roll(state[f, 1], LANES // 2, 1), state[f, 0]
        )
    for copy in outers:
        copy.start()
    for f in range(fields):
        for x in range(2):
            ext[f, x, pl.ds(RIM, cells), :] = state[f, x]
    for copy in halos:
        copy.wait_recv()

    def turned(ref, c, sign):
        if c < 4:
            window = pl.ds((c % 2) * half, half)
            u, v = turn[0, window, :], turn[1, window, :]
        else:
            u = jnp.where(low_lanes, turn[0, pl.ds(0, half), :], turn[0, pl.ds(half, half), :])
            v = jnp.where(low_lanes, turn[1, pl.ds(0, half), :], turn[1, pl.ds(half, half), :])
        v = v * sign
        cosine, sine = ref[c, 0], ref[c, 1]
        return u * cosine + v * sine, u * sine - v * cosine

    def relay(c):
        @pl.when(jnp.logical_not(is_first))
        def _():
            rights[c].wait_recv()

        @pl.when(jnp.logical_not(is_first) & jnp.logical_not(is_last))
        def _():
            cosine, sine = turned(from_left, c, 1.0)
            to_right[c, 0] = own[c, 0] + cosine
            to_right[c, 1] = own[c, 1] + sine
            rights[c].start()

        @pl.when(jnp.logical_not(is_last))
        def _():
            lefts[c].wait_recv()

        @pl.when(jnp.logical_not(is_first) & jnp.logical_not(is_last))
        def _():
            cosine, sine = turned(from_right, c, -1.0)
            to_left[c, 0] = own[c, 0] + cosine
            to_left[c, 1] = own[c, 1] + sine
            lefts[c].start()

        @pl.when(jnp.logical_not(is_first))
        def _():
            cosine, sine = turned(from_left, c, 1.0)
            own[c, 0] = own[c, 0] + cosine
            own[c, 1] = own[c, 1] + sine

        @pl.when(jnp.logical_not(is_last))
        def _():
            cosine, sine = turned(from_right, c, -1.0)
            own[c, 0] = own[c, 0] + cosine
            own[c, 1] = own[c, 1] + sine

    lane_tall = lax.broadcasted_iota(jnp.int32, (tall, LANES), 1)
    parity_tall = (1 - 2 * (lax.broadcasted_iota(jnp.int32, (tall, LANES), 0) & 1)).astype(F32)

    def restore(tile):
        for side in range(2):
            row = row_ids + side * half
            back_row = rows - 1 - row
            top_weight = jnp.where(row < top_keep, jnp.where(row == 0, 1.0 / NTH, 2.0 / NTH), 0.0)
            bottom_weight = jnp.where(
                back_row < bottom_keep, jnp.where(back_row == 0, 1.0 / NTH, 2.0 / NTH), 0.0
            )
            flips = (1 - 2 * (back_row & 1)).astype(F32)
            if tile == 2:
                mine = low_lanes if side == 0 else jnp.logical_not(low_lanes)
                top_weight = jnp.where(mine, top_weight, 0.0)
                bottom_weight = jnp.where(mine, bottom_weight, 0.0)
            for part in range(2):
                waves = own[2 * tile + side, part] if tile < 2 else own[4, part]
                window = pl.ds(part * rows + side * half, half)
                top_high, top_low = split(waves * top_weight)
                weighted = waves * bottom_weight
                bottom_high, bottom_low = split(weighted)
                far_high, far_low = split(weighted * flips)
                spectrum[0, window, :] = top_high
                spectrum[1, window, :] = top_low
                spectrum[2, window, :] = bottom_high
                spectrum[3, window, :] = bottom_low
                spectrum[4, window, :] = far_high
                spectrum[5, window, :] = far_low

        def series(which, base):
            return (
                mm(inverse[which, 0], spectrum[base])
                + mm(inverse[which, 0], spectrum[base + 1])
                + mm(inverse[which, 1], spectrum[base])
            )

        near = split(jnp.concatenate([series(0, 0), series(1, 2)], axis=1))
        far = split(series(1, 4))
        for item, slot in tile_items(tile):
            f, x = item // 2, item % 2
            filtered = mm(near[0], back[slot]) + mm(near[1], back[slot])
            across = mm(far[0], ghost[slot]) + mm(far[1], ghost[slot])
            raw = ext[f, x]
            cells_now = jnp.where(lane_tall >= first_dropped, raw - parity_tall * filtered, filtered)
            across = -across if f in (2, 3) else across
            ext[f, x] = jnp.where(lane_tall >= LANES - 2, across, cells_now)
            if x == 1:
                centre = pl.ds(RIM, cells)
                inner_own[f] = jnp.where(
                    lane_cells < LANES // 2,
                    ext[f, 0, centre, :],
                    pltpu.roll(ext[f, 1, centre, :], LANES // 2, 1),
                )
                for copy in inners[f]:
                    copy.start()

    relay(0)
    relay(1)
    relay(2)
    restore(0)
    relay(3)
    restore(1)
    relay(4)
    restore(2)

    block = min(32, cells)
    deep = block + 2 * RIM
    lane_deep = lax.broadcasted_iota(jnp.int32, (deep, LANES), 1)
    lane_block = lax.broadcasted_iota(jnp.int32, (block, LANES), 1)
    radius = jnp.where(lane_block >= LANES - 2, lane_block - LANES, lane_block).astype(F32) + 0.5
    inv_radius = 1.0 / radius
    angular = inv_radius * (1.0 / (12.0 * (2.0 * math.pi / NTH)))
    radial = inv_radius * (1.0 / 12.0)

    @pl.loop(0, 2 * (cells // block))
    def _(step):
        x = step % 2
        start = pl.multiple_of((step // 2) * block, block)
        values = [ext[f, x, pl.ds(start, deep), :] for f in range(fields)]
        around, _, _ = fluxes(values, 3)
        centre = [value[RIM : RIM + block] for value in values]
        outward, inverse_density, pressure = fluxes(centre, 2)
        sources = [
            None,
            None,
            (centre[3] * centre[3] * inverse_density + pressure) * inv_radius,
            -(centre[2] * centre[3] * inverse_density) * inv_radius,
            None,
        ]
        for f in range(fields):
            g = around[f]
            turn_term = (
                8.0 * (pltpu.roll(g, deep - 1, 0) - pltpu.roll(g, 1, 0))
                - (pltpu.roll(g, deep - 2, 0) - pltpu.roll(g, 2, 0))
            )[RIM : RIM + block]
            g = outward[f] * radius
            out_term = 8.0 * (pltpu.roll(g, LANES - 1, 1) - pltpu.roll(g, 1, 1)) - (
                pltpu.roll(g, LANES - 2, 1) - pltpu.roll(g, 2, 1)
            )
            total = -(turn_term * angular + out_term * radial)
            if sources[f] is not None:
                total = total + sources[f]
            out[f, x, pl.ds(start, block), :] = (STEP_DT * total)[:, :cycles]

    for copy in outers:
        copy.wait_recv()
    for pair in inners:
        for copy in pair:
            copy.wait_recv()

    low_block = lane_block < LANES // 2

    @pl.loop(0, cells // block)
    def _(step):
        window = pl.ds(pl.multiple_of(step * block, block), block)

        def axial_term(mid, left, right, swapped):
            mids = fluxes([mid[f, window, :] for f in range(fields)], 1)[0]
            lefts_ = fluxes([left[f, window, :] for f in range(fields)], 1)[0]
            rights_ = fluxes([right[f, window, :] for f in range(fields)], 1)[0]
            terms = []
            for f in range(fields):
                back_step, fore_step = mids[f] - lefts_[f], rights_[f] - mids[f]
                if swapped:
                    mixed = jnp.where(low_block, back_step, fore_step)
                else:
                    mixed = jnp.where(low_block, fore_step, back_step)
                terms.append(8.0 * pltpu.roll(mixed, LANES // 2, 1) - (rights_[f] - lefts_[f]))
            return terms

        inner = axial_term(inner_own, inner_left, inner_right, False)
        outer = axial_term(outer_own, outer_left, outer_right, True)
        for f in range(fields):
            first = jnp.where(low_block, inner[f], outer[f])
            second = pltpu.roll(jnp.where(low_block, outer[f], inner[f]), LANES // 2, 1)
            for x, term in ((0, first), (1, second)):
                out[f, x, window, :] = out[f, x, window, :] - (STEP_DT / 12.0) * term[:, :cycles]

    for copy in halos + outers:
        copy.wait_send()
    for pair in inners:
        for copy in pair:
            copy.wait_send()
    for c in range(chunks):
        @pl.when(jnp.logical_not(is_last))
        def _():
            rights[c].wait_send()

        @pl.when(jnp.logical_not(is_first))
        def _():
            lefts[c].wait_send()


def shards(state, start, modes):
    fields, axial, cells, cycles = state.shape
    cfg = plan(cells)
    rows, half = cfg["rows"], cfg["rows"] // 2
    counts = jnp.where(
        np.arange(NIN) < cfg["first_dropped"], modes, NTH // 2 + 1 - modes
    ).astype(jnp.int32)
    limits = jnp.stack(
        [
            jnp.tile(counts[cfg["top"]], cfg["slots"]),
            jnp.tile(counts[cfg["bottom"]], cfg["slots"]),
            jnp.asarray(cfg["top_rows"]),
        ]
    )
    padded = jnp.pad(state, ((0, 0), (0, 0), (0, 0), (0, LANES - cycles)), mode="edge")
    plane = (fields, cells, LANES)
    chunk = (5, 2, half, LANES)
    vmem = pl.BlockSpec(memory_space=pltpu.VMEM)
    step = pl.pallas_call(
        functools.partial(kernel, cfg),
        out_shape=jax.ShapeDtypeStruct(state.shape, F32),
        in_specs=[vmem] * 8,
        out_specs=vmem,
        scratch_shapes=[pltpu.VMEM((fields, axial, cells + 2 * RIM, LANES), F32)]
        + [pltpu.VMEM(plane, F32)] * 6
        + [pltpu.VMEM(chunk, F32)] * 5
        + [pltpu.VMEM((6, 2 * rows, LANES), BF16)]
        + [
            pltpu.SemaphoreType.DMA((2,)),
            pltpu.SemaphoreType.DMA((2,)),
            pltpu.SemaphoreType.DMA((2,)),
            pltpu.SemaphoreType.DMA((2,)),
            pltpu.SemaphoreType.DMA((2, fields)),
            pltpu.SemaphoreType.DMA((2, fields)),
            pltpu.SemaphoreType.DMA((2, 5)),
            pltpu.SemaphoreType.DMA((2, 5)),
        ],
        compiler_params=pltpu.CompilerParams(
            collective_id=0, has_side_effects=True, vmem_limit_bytes=48 * 1024 * 1024
        ),
        name="jet_section",
    )(
        padded,
        limits,
        jnp.asarray(cfg["forward"]),
        jnp.asarray(cfg["inverse"]),
        jnp.asarray(cfg["place"]),
        jnp.asarray(cfg["back"]),
        jnp.asarray(cfg["ghost"]),
        jnp.asarray(cfg["turn"]),
    )
    return start + step


def solution(mesh):
    in_specs = (P(None, "axial", "azim", None), P(None, "axial", "azim", None), P())
    out_specs = P(None, "axial", "azim", None)
    return jax.shard_map(shards, mesh=mesh, in_specs=in_specs, out_specs=out_specs, check_vma=False)
```

time: 145 us -> 96.1 us (0.66)
  Pallas kernels: 0 us -> 81.4 us
  waiting for transfers between devices: 63.5 us -> 0 us
  local copies, waits for them, and re-layouts: 41.6 us -> 8.55 us
  other arithmetic: 21.3 us -> 4.6 us
  starting transfers between devices: 13.5 us -> 0 us
  matrix products: 3.72 us -> 0 us
    pallas_call x0 -> x1, Pallas kernels: none -> 81.4 us  [shards(): pl.pallas_call(functools.partial(kernel, cfg), out_shape=jax.ShapeDtypeSt...]
    all_to_all x2 -> x0, waiting for transfers between devices: 39.2 us -> none  [the longest x1 23.5 us: shards(): lax.all_to_all(inner, 'azim', split_axis=1, concat_axis=2, tiled=True)]
    ppermute x5 -> x0, waiting for transfers between devices: 24.3 us -> none  [the longest x2 17.2 us: with_halo(): lax.ppermute(head, axis, [((i + 1) % count, i) for i in range(count)])]
    unnamed x40 -> x15, local copies, waits for them, and re-layouts: 17.9 us -> 4.35 us
    all_to_all x2 -> x0, starting transfers between devices: 10 us -> none  [the longest x1 6.35 us: shards(): lax.all_to_all(inner, 'azim', split_axis=1, concat_axis=2, tiled=True)]
    slice x7 -> x1, local copies, waits for them, and re-layouts: 8.43 us -> 0.9 us  [shards(): jnp.pad(state, ((0, 0), (0, 0), (0, 0), (0, LANES - cycles)), mode='edge')]
    concatenate x3 -> x1, other arithmetic: 7.39 us -> 0.41 us  [shards(): jnp.pad(state, ((0, 0), (0, 0), (0, 0), (0, LANES - cycles)), mode='edge')]
    all_to_all x4 -> x0, local copies, waits for them, and re-layouts: 6.51 us -> none  [the longest x3 6.09 us: shards(): lax.all_to_all(smoothed, 'azim', split_axis=2, concat_axis=1, tiled=True)]
  transfers between devices with their start and end apart: 7 -> 0, of which waited for: 6 -> 0; matrix products, arithmetic and copies ran while one was open for 7% -> 0% of each run, Pallas kernels for 0% -> 0%
where the time goes in v2:
time: 96.1 us; the launch traced here: 94.7 us
  Pallas kernels  81.4 us (85%)
  local copies, waits for them, and re-layouts  8.55 us (9%)
  other arithmetic  4.6 us (5%)
    pallas_call x1, Pallas kernels, shards(): pl.pallas_call(functools.partial(kernel, cfg), out_shape=jax.ShapeDtypeSt...  81.4 us
    unnamed x15, local copies, waits for them, and re-layouts  4.35 us

profile of v2, /device:TPU:0, one launch (start us, length us, event | category | flops | bytes accessed | tf_op | source)
XLA Modules:
  0.0 94.7 jit_solution(15537552976094979630)
XLA Ops:
  0.0 0.7 subtract_select_fusion
  0.7 0.7 pad_clamp_fusion.1
  1.3 0.7 gather_fusion
  2.0 0.1 stack_tile.6
  2.1 0.7 pad_clamp_fusion
  2.8 0.7 gather_fusion.1
  3.5 0.1 stack_tile.7
  3.6 0.7 pad_add_fusion.limits
  4.3 0.9 slice.6
  5.2 0.4 reshape.7
  5.6 1.6 %copy.22 = f32[5,2,256,96]{3,2,1,0:T(8,128)S(1)} copy(f32[5,2,256,96]{2,3,1,0:T(8,128)} %param.15) | data formatting | bytes 1966080 | tf_op args[0]
  7.2 0.0 copy-start
  7.2 0.0 copy-start.1
  7.2 0.0 copy-start.2
  7.2 0.0 copy-start.3
  7.2 0.0 copy-start.4
  7.2 0.4 pad_maximum_fusion.state
  7.7 0.9 copy-done
  8.5 0.1 copy-done.1
  8.6 0.1 copy-done.2
  8.7 0.1 copy-done.3
  8.8 0.1 copy-done.4
  8.9 0.0 copy-start.5
  8.9 81.4 %jet_section.1 = f32[5,2,256,96]{3,2,1,0:T(8,128)S(1)} custom-call(f32[5,2,256,128]{3,2,1,0:T(8,128)S(1)} %pad_maximum_fusion.state, s32[3,128]{1,0:T(4,128)S(1)} %pad_add_fusion.limits, bf16[2,2,704,256]{3,2,1,0:T(8,128)(2,1)S(1)} %copy-done, bf16[2,2,272,704]{3,2,1,0:T(8,128)(2,1)} %constant.32.clone.inverse, bf16[6,128,256]{2,1,0:T(8,128)(2,1)S(1)} %copy-done.1, ...), custom_call_target="tpu_custom_call" | custom-call | tf_op jit(solution)/shard_map/jet_section/pallas_call | solution.py:458
  90.3 0.0 copy-done.5
  90.3 1.5 %copy.23 = f32[5,2,256,96]{3,2,1,0:T(8,128)} copy(f32[5,2,256,96]{2,3,1,0:T(8,128)S(1)} %copy-done.5) | data formatting | bytes 1966080 | tf_op args[1]
  91.8 1.5 %add.11 = f32[5,2,256,96]{3,2,1,0:T(8,128)S(1)} add(f32[5,2,256,96]{3,2,1,0:T(8,128)} %copy.23, f32[5,2,256,96]{3,2,1,0:T(8,128)S(1)} %jet_section.1) | non-fusion elementwise | flops 245760 | bytes 2949120 | tf_op jit(solution)/shard_map/add | solution.py:491
  93.3 1.3 %copy.24 = f32[5,2,256,96]{2,3,1,0:T(8,128)} copy(f32[5,2,256,96]{3,2,1,0:T(8,128)S(1)} %add.11) | data formatting | bytes 1966080 | tf_op jit(solution)/shard_map/add | solution.py:491
  (3 shorter events, 0.0 us)
Async XLA Ops:
  7.2 1.4 %copy-start = (bf16[2,2,704,256]{3,2,1,0:T(8,128)(2,1)S(1)}, bf16[2,2,704,256]{3,2,1,0:T(8,128)(2,1)}, u32[]{:S(2)}) copy-start(bf16[2,2,704,256]{3,2,1,0:T(8,128)(2,1)} %constant.31.clone.forward) | copy-start | bytes 4325380
  7.2 1.4 %copy-start.1 = (bf16[6,128,256]{2,1,0:T(8,128)(2,1)S(1)}, bf16[6,128,256]{2,1,0:T(8,128)(2,1)}, u32[]{:S(2)}) copy-start(bf16[6,128,256]{2,1,0:T(8,128)(2,1)} %constant.33.clone.place) | copy-start | bytes 1179652
  7.2 1.5 %copy-start.2 = (bf16[6,256,128]{2,1,0:T(8,128)(2,1)S(1)}, bf16[6,256,128]{2,1,0:T(8,128)(2,1)}, u32[]{:S(2)}) copy-start(bf16[6,256,128]{2,1,0:T(8,128)(2,1)} %constant.34.clone.back) | copy-start | bytes 1179652
  7.2 1.6 %copy-start.3 = (f32[2,352,128]{2,1,0:T(8,128)S(1)}, f32[2,352,128]{2,1,0:T(8,128)}, u32[]{:S(2)}) copy-start(f32[2,352,128]{2,1,0:T(8,128)} %constant.36.clone.turn) | copy-start | bytes 1081348
  7.2 1.7 %copy-start.4 = (bf16[6,128,128]{2,1,0:T(8,128)(2,1)S(1)}, bf16[6,128,128]{2,1,0:T(8,128)(2,1)}, u32[]{:S(2)}) copy-start(bf16[6,128,128]{2,1,0:T(8,128)(2,1)} %constant.35.clone.ghost) | copy-start | bytes 589828
  8.9 81.4 %copy-start.5 = (f32[5,2,256,96]{2,3,1,0:T(8,128)S(1)}, f32[5,2,256,96]{2,3,1,0:T(8,128)}, u32[]{:S(2)}) copy-start(f32[5,2,256,96]{2,3,1,0:T(8,128)} %param.16) | copy-start | bytes 2949124

commit v3 on v2

v3 whole, which is shorter than its diff:
```python
import functools
import math

import jax
import jax.numpy as jnp
import numpy as np
from jax import lax
from jax.experimental import pallas as pl
from jax.experimental.pallas import tpu as pltpu
from jax.sharding import PartitionSpec as P

NTH = 1024
NIN = 64
MSTEP = 8
STEP_DT = 0.05
LANES = 128
RIM = 8
F32 = jnp.float32
BF16 = jnp.bfloat16
MESH = pl.DeviceIdType.MESH


def split_np(values):
    high = values.astype(np.float32).astype(jnp.bfloat16)
    low = (values - high.astype(np.float64)).astype(np.float32).astype(jnp.bfloat16)
    return np.stack([high, low])


@functools.lru_cache(None)
def plan(cells):
    order = np.arange(1, NIN + 1)
    kept = np.minimum(2 * MSTEP * order, NTH // 2)
    dropped = NTH // 2 + 1 - np.minimum(MSTEP * order, NTH // 2)
    use_kept = kept <= dropped
    bound = np.where(use_kept, kept, dropped)
    first_dropped = int(np.argmin(use_kept))
    ranked = np.argsort(-bound, kind="stable")
    pairs = NIN // 2
    top, bottom = ranked[:pairs], ranked[::-1][:pairs]
    rows = int(-(-np.max(bound[top] + bound[bottom]) // 32) * 32)
    wave = np.arange(rows)
    angle = lambda n, q: 2 * np.pi * ((n * q) % NTH) / NTH
    forward = []
    for waves in (wave, wave[::-1]):
        phase = angle(np.arange(cells)[None, :], waves[:, None])
        forward.append(split_np(np.concatenate([np.cos(phase), np.sin(phase)], 0)))
    inverse = []
    for waves in (wave, wave[::-1]):
        phase = angle(np.arange(-RIM, cells + RIM)[:, None], waves[None, :])
        inverse.append(split_np(np.concatenate([np.cos(phase), np.sin(phase)], 1)))
    slots = LANES // pairs
    place = np.zeros((slots + slots // 2, LANES, 2 * LANES), np.float32)
    ghost = np.zeros((slots + slots // 2, LANES, LANES), np.float32)
    for slot in range(slots):
        for pair in range(pairs):
            place[slot, top[pair], slot * pairs + pair] = 1
            place[slot, bottom[pair], LANES + slot * pairs + pair] = 1
            if bottom[pair] < 2:
                ghost[slot, slot * pairs + pair, LANES - 1 - bottom[pair]] = 1
    half = slots // 2
    for k in range(half):
        place[slots + k] = place[k] + place[half + k]
        ghost[slots + k] = ghost[k] + ghost[half + k]
    far_rows = int(-(-np.max(bound[:2]) // 16) * 16)
    far_phase = angle(
        np.arange(-RIM, cells + RIM)[:, None] + NTH // 2, np.arange(far_rows)[::-1][None, :]
    )
    far = split_np(np.concatenate([np.cos(far_phase), np.sin(far_phase)], 1))
    groups = (slots + half) // 2
    back = place.transpose(0, 2, 1)
    back = back.reshape(groups, 2, 2 * LANES, LANES).transpose(0, 2, 1, 3)
    ghost = ghost.reshape(groups, 2, LANES, LANES).transpose(0, 2, 1, 3)
    top_rows = np.tile(bound[top], slots)
    wave_of = np.where(wave[:, None] < top_rows[None, :], wave[:, None], rows - 1 - wave[:, None])
    turn = angle(cells, wave_of)
    return dict(
        rows=rows,
        far_rows=far_rows,
        far=far,
        first_dropped=first_dropped,
        top_rows=top_rows.astype(np.int32)[None],
        forward=np.stack(forward),
        inverse=np.stack(inverse),
        place=place.reshape(groups, 2 * LANES, 2 * LANES).astype(jnp.bfloat16),
        back=back.reshape(groups, 2 * LANES, 2 * LANES).astype(jnp.bfloat16),
        ghost=ghost.reshape(groups, LANES, 2 * LANES).astype(jnp.bfloat16),
        turn=np.stack([np.cos(turn), np.sin(turn)]).astype(np.float32),
    )


def split(values):
    high = values.astype(BF16)
    return high, (values - high.astype(F32)).astype(BF16)


def mm(a, b):
    return jnp.dot(a, b, preferred_element_type=F32)


def fluxes(values, direction):
    inverse = 1.0 / values[0]
    velocity = values[direction] * inverse
    kinetic = (values[1] * values[1] + values[2] * values[2] + values[3] * values[3]) * inverse
    pressure = 0.4 * (values[4] - 0.5 * kinetic)
    parts = [
        values[direction],
        values[1] * velocity,
        values[2] * velocity,
        values[3] * velocity,
        (values[4] + pressure) * velocity,
    ]
    parts[direction] = parts[direction] + pressure
    return parts, inverse, pressure


def kernel(
    cfg,
    state, modes, bounds, forward, inverse, place, back, ghost, turn, far_table,
    out,
    ext, rate, outer_own, outer_left, outer_right, inner_own, inner_left, inner_right,
    own, to_right, to_left, from_left, from_right, spectrum,
    halo_send, halo_recv, outer_send, outer_recv, inner_send, inner_recv, wave_send, wave_recv,
):
    rows, first_dropped = cfg["rows"], cfg["first_dropped"]
    half, quarter = rows // 2, rows // 4
    far_rows = cfg["far_rows"]
    fields, cycles, cells = state.shape[0], state.shape[2], state.shape[3]
    tall = cells + 2 * RIM
    d, count = lax.axis_index("azim"), lax.axis_size("azim")
    a, ring = lax.axis_index("axial"), lax.axis_size("axial")
    z_right = {"azim": lax.rem(d + 1, count)}
    z_left = {"azim": lax.rem(d + count - 1, count)}
    x_right = {"axial": lax.rem(a + 1, ring)}
    x_left = {"axial": lax.rem(a + ring - 1, ring)}

    def remote(src, dst, send, recv, device):
        return pltpu.make_async_remote_copy(
            src_ref=src, dst_ref=dst, send_sem=send, recv_sem=recv,
            device_id=device, device_id_type=MESH,
        )

    barrier = pltpu.get_barrier_semaphore()
    for device in (z_right, z_left, x_right, x_left):
        pl.semaphore_signal(barrier, inc=1, device_id=device, device_id_type=MESH)
    for f in range(fields):
        for x in range(2):
            value = state[f, x]
            tail = jnp.broadcast_to(value[cycles - 1 :], (LANES - cycles, cells))
            ext[f, x, pl.ds(RIM, cells), :] = jnp.concatenate([value, tail], axis=0).T
    for f in range(fields):
        low_lane = lax.broadcasted_iota(jnp.int32, (cells, LANES), 1) < LANES // 2
        outer_own[f] = jnp.where(
            low_lane,
            pltpu.roll(ext[f, 1, pl.ds(RIM, cells), :], LANES // 2, 1),
            ext[f, 0, pl.ds(RIM, cells), :],
        )
    pl.semaphore_wait(barrier, 4)

    halos = [
        remote(
            ext.at[:, :, pl.ds(cells, RIM)], ext.at[:, :, pl.ds(0, RIM)],
            halo_send.at[0], halo_recv.at[0], z_right,
        ),
        remote(
            ext.at[:, :, pl.ds(RIM, RIM)], ext.at[:, :, pl.ds(cells + RIM, RIM)],
            halo_send.at[1], halo_recv.at[1], z_left,
        ),
    ]
    outers = [
        remote(outer_own, outer_left, outer_send.at[0], outer_recv.at[0], x_right),
        remote(outer_own, outer_right, outer_send.at[1], outer_recv.at[1], x_left),
    ]
    chunks = 10
    rights = [
        remote(to_right.at[c], from_left.at[c], wave_send.at[0, c], wave_recv.at[0, c], z_right)
        for c in range(chunks)
    ]
    lefts = [
        remote(to_left.at[c], from_right.at[c], wave_send.at[1, c], wave_recv.at[1, c], z_left)
        for c in range(chunks)
    ]
    inners = [
        [
            remote(inner_own.at[f], inner_left.at[f], inner_send.at[0, f], inner_recv.at[0, f], x_right),
            remote(inner_own.at[f], inner_right.at[f], inner_send.at[1, f], inner_recv.at[1, f], x_left),
        ]
        for f in range(fields)
    ]
    is_first, is_last = d == 0, d == count - 1

    lane_cells = lax.broadcasted_iota(jnp.int32, (cells, LANES), 1)
    parity_cells = (1 - 2 * (lax.broadcasted_iota(jnp.int32, (cells, LANES), 0) & 1)).astype(F32)
    signs = jnp.where(lane_cells >= first_dropped, parity_cells, 1.0)
    row_ids = lax.broadcasted_iota(jnp.int32, (quarter, LANES), 0)
    low_lanes = lax.broadcasted_iota(jnp.int32, (quarter, LANES), 1) < LANES // 2
    top_rows = bounds[...]
    cycle_ids = lax.broadcasted_iota(jnp.int32, (8, NIN), 1)
    kept_modes = jnp.broadcast_to(modes[...], (8, NIN))
    counts = split(
        jnp.where(cycle_ids < first_dropped, kept_modes, NTH // 2 + 1 - kept_modes).astype(F32)
    )
    last = place.shape[0] - 1
    keep = sum(
        mm(term, place[last, pl.ds(first, NIN), :]) for term in counts for first in (0, LANES)
    )
    top_keep, bottom_keep = keep[0:1, :LANES], keep[0:1, LANES:]

    def tile_fields(tile):
        if tile < 2:
            return [(2 * tile, 0), (2 * tile + 1, 1)]
        return [(4, 2)]

    def tile_chunks(tile):
        return range(4 * tile, 4 * tile + 4) if tile < 2 else range(8, 10)

    for copy in halos + outers:
        copy.start()
    for tile in range(3):
        high = jnp.zeros((cells, 2 * LANES), F32)
        low = jnp.zeros((cells, 2 * LANES), F32)
        for f, group in tile_fields(tile):
            planes = [ext[f, x, pl.ds(RIM, cells), :] * signs for x in range(2)]
            field_high, field_low = split(jnp.concatenate(planes, axis=1))
            high = high + mm(field_high, place[group])
            low = low + mm(field_low, place[group])
        high, low = high.astype(BF16), low.astype(BF16)
        for part in range(2):
            window = pl.ds(part * rows, rows)
            sums = []
            for which in range(2):
                lanes = slice(which * LANES, (which + 1) * LANES)
                both = mm(
                    forward[which, 0, window, :],
                    jnp.concatenate([high[:, lanes], low[:, lanes]], axis=1),
                )
                sums.append(
                    both[:, :LANES]
                    + both[:, LANES:]
                    + mm(forward[which, 1, window, :], high[:, lanes])
                )
            pieces = []
            for side in range(4):
                part_rows = slice(side * quarter, (side + 1) * quarter)
                pieces.append(
                    jnp.where(
                        row_ids + side * quarter < top_rows, sums[0][part_rows], sums[1][part_rows]
                    )
                )
            for k, c in enumerate(tile_chunks(tile)):
                own[c, part] = pieces[k] if tile < 2 else jnp.where(low_lanes, pieces[k], pieces[k + 2])
        for c in tile_chunks(tile):
            @pl.when(is_first)
            def _():
                to_right[c] = own[c]
                rights[c].start()

            @pl.when(is_last)
            def _():
                to_left[c] = own[c]
                lefts[c].start()

    for copy in halos:
        copy.wait()

    def turned(ref, c, sign):
        if c < 8:
            window = pl.ds((c % 4) * quarter, quarter)
            u, v = turn[0, window, :], turn[1, window, :]
        else:
            low_window = pl.ds((c - 8) * quarter, quarter)
            high_window = pl.ds(half + (c - 8) * quarter, quarter)
            u = jnp.where(low_lanes, turn[0, low_window, :], turn[0, high_window, :])
            v = jnp.where(low_lanes, turn[1, low_window, :], turn[1, high_window, :])
        v = v * sign
        cosine, sine = ref[c, 0], ref[c, 1]
        return u * cosine + v * sine, u * sine - v * cosine

    inside = jnp.logical_not(is_first) & jnp.logical_not(is_last)
    near_first = 2 * d < count

    def pass_right(c, when):
        @pl.when(when & jnp.logical_not(is_first))
        def _():
            rights[c].wait_recv()

        @pl.when(when & inside)
        def _():
            cosine, sine = turned(from_left, c, 1.0)
            to_right[c, 0] = own[c, 0] + cosine
            to_right[c, 1] = own[c, 1] + sine
            rights[c].start()

    def relay(c):
        pass_right(c, near_first)

        @pl.when(jnp.logical_not(is_last))
        def _():
            lefts[c].wait_recv()

        @pl.when(inside)
        def _():
            cosine, sine = turned(from_right, c, -1.0)
            to_left[c, 0] = own[c, 0] + cosine
            to_left[c, 1] = own[c, 1] + sine
            lefts[c].start()

        pass_right(c, jnp.logical_not(near_first))

        @pl.when(jnp.logical_not(is_first))
        def _():
            cosine, sine = turned(from_left, c, 1.0)
            own[c, 0] = own[c, 0] + cosine
            own[c, 1] = own[c, 1] + sine

        @pl.when(jnp.logical_not(is_last))
        def _():
            cosine, sine = turned(from_right, c, -1.0)
            own[c, 0] = own[c, 0] + cosine
            own[c, 1] = own[c, 1] + sine

    lane_tall = lax.broadcasted_iota(jnp.int32, (tall, LANES), 1)
    parity_tall = (1 - 2 * (lax.broadcasted_iota(jnp.int32, (tall, LANES), 0) & 1)).astype(F32)

    def restore(tile):
        for side in range(4):
            row = row_ids + side * quarter
            back_row = rows - 1 - row
            top_weight = jnp.where(
                row.astype(F32) < top_keep, jnp.where(row == 0, 1.0 / NTH, 2.0 / NTH), 0.0
            )
            bottom_weight = jnp.where(
                back_row.astype(F32) < bottom_keep,
                jnp.where(back_row == 0, 1.0 / NTH, 2.0 / NTH),
                0.0,
            )
            if tile == 2:
                mine = low_lanes if side < 2 else jnp.logical_not(low_lanes)
                top_weight = jnp.where(mine, top_weight, 0.0)
                bottom_weight = jnp.where(mine, bottom_weight, 0.0)
            c = 4 * tile + side if tile < 2 else 8 + side % 2
            for part in range(2):
                waves = own[c, part]
                window = pl.ds(part * rows + side * quarter, quarter)
                for which, weight in ((0, top_weight), (1, bottom_weight)):
                    weighted = split(waves * weight)
                    spectrum[which, window, pl.ds(0, LANES)] = weighted[0]
                    spectrum[which, window, pl.ds(LANES, LANES)] = weighted[1]

        def series(which):
            both = mm(inverse[which, 0], spectrum[which])
            return (
                both[:, :LANES]
                + both[:, LANES:]
                + mm(inverse[which, 1], spectrum[which, :, pl.ds(0, LANES)])
            )

        near = split(jnp.concatenate([series(0), series(1)], axis=1))
        waves = jnp.concatenate(
            [spectrum[1, pl.ds((part + 1) * rows - far_rows, far_rows), :] for part in range(2)],
            axis=0,
        )
        both = mm(far_table[0], waves)
        far = split(both[:, :LANES] + both[:, LANES:] + mm(far_table[1], waves[:, :LANES]))
        for f, group in tile_fields(tile):
            filtered = mm(near[0], back[group]) + mm(near[1], back[group])
            across = mm(far[0], ghost[group]) + mm(far[1], ghost[group])
            across = -across if f in (2, 3) else across
            for x in range(2):
                lanes = slice(x * LANES, (x + 1) * LANES)
                raw = ext[f, x]
                now = jnp.where(
                    lane_tall >= first_dropped,
                    raw - parity_tall * filtered[:, lanes],
                    filtered[:, lanes],
                )
                ext[f, x] = jnp.where(lane_tall >= LANES - 2, across[:, lanes], now)
            centre = pl.ds(RIM, cells)
            inner_own[f] = jnp.where(
                lane_cells < LANES // 2,
                ext[f, 0, centre, :],
                pltpu.roll(ext[f, 1, centre, :], LANES // 2, 1),
            )
            for copy in inners[f]:
                copy.start()

    for c in range(5):
        relay(c)
    restore(0)
    for c in range(5, 9):
        relay(c)
    restore(1)
    relay(9)
    restore(2)

    block = min(32, cells)
    deep = block + 2 * RIM
    lane_deep = lax.broadcasted_iota(jnp.int32, (deep, LANES), 1)
    lane_block = lax.broadcasted_iota(jnp.int32, (block, LANES), 1)
    radius = jnp.where(lane_block >= LANES - 2, lane_block - LANES, lane_block).astype(F32) + 0.5
    inv_radius = 1.0 / radius
    angular = inv_radius * (1.0 / (12.0 * (2.0 * math.pi / NTH)))
    radial = inv_radius * (1.0 / 12.0)

    @pl.loop(0, 2 * (cells // block))
    def _(step):
        x = step % 2
        start = pl.multiple_of((step // 2) * block, block)
        values = [ext[f, x, pl.ds(start, deep), :] for f in range(fields)]
        around, _, _ = fluxes(values, 3)
        centre = [value[RIM : RIM + block] for value in values]
        outward, inverse_density, pressure = fluxes(centre, 2)
        sources = [
            None,
            None,
            (centre[3] * centre[3] * inverse_density + pressure) * inv_radius,
            -(centre[2] * centre[3] * inverse_density) * inv_radius,
            None,
        ]
        for f in range(fields):
            g = around[f]
            turn_term = (
                8.0 * (pltpu.roll(g, deep - 1, 0) - pltpu.roll(g, 1, 0))
                - (pltpu.roll(g, deep - 2, 0) - pltpu.roll(g, 2, 0))
            )[RIM : RIM + block]
            g = outward[f] * radius
            out_term = 8.0 * (pltpu.roll(g, LANES - 1, 1) - pltpu.roll(g, 1, 1)) - (
                pltpu.roll(g, LANES - 2, 1) - pltpu.roll(g, 2, 1)
            )
            total = -(turn_term * angular + out_term * radial)
            if sources[f] is not None:
                total = total + sources[f]
            rate[f, x, pl.ds(start, block), :] = STEP_DT * total

    for copy in outers:
        copy.wait_recv()
    for pair in inners:
        for copy in pair:
            copy.wait_recv()

    low_block = lane_block < LANES // 2

    @pl.loop(0, cells // block)
    def _(step):
        window = pl.ds(pl.multiple_of(step * block, block), block)

        def axial_term(mid, left, right, swapped):
            mids = fluxes([mid[f, window, :] for f in range(fields)], 1)[0]
            lefts_ = fluxes([left[f, window, :] for f in range(fields)], 1)[0]
            rights_ = fluxes([right[f, window, :] for f in range(fields)], 1)[0]
            terms = []
            for f in range(fields):
                back_step, fore_step = mids[f] - lefts_[f], rights_[f] - mids[f]
                if swapped:
                    mixed = jnp.where(low_block, back_step, fore_step)
                else:
                    mixed = jnp.where(low_block, fore_step, back_step)
                terms.append(8.0 * pltpu.roll(mixed, LANES // 2, 1) - (rights_[f] - lefts_[f]))
            return terms

        inner = axial_term(inner_own, inner_left, inner_right, False)
        outer = axial_term(outer_own, outer_left, outer_right, True)
        for f in range(fields):
            first = jnp.where(low_block, inner[f], outer[f])
            second = pltpu.roll(jnp.where(low_block, outer[f], inner[f]), LANES // 2, 1)
            for x, term in ((0, first), (1, second)):
                rate[f, x, window, :] = rate[f, x, window, :] - (STEP_DT / 12.0) * term

    for f in range(fields):
        for x in range(2):
            out[f, x] = rate[f, x].T[:cycles]

    for copy in outers:
        copy.wait_send()
    for pair in inners:
        for copy in pair:
            copy.wait_send()
    for c in range(chunks):
        @pl.when(jnp.logical_not(is_last))
        def _():
            rights[c].wait_send()

        @pl.when(jnp.logical_not(is_first))
        def _():
            lefts[c].wait_send()


def shards(state, start, modes):
    fields, axial, cells, cycles = state.shape
    cfg = plan(cells)
    rows = cfg["rows"]
    turned = state.transpose(0, 1, 3, 2)
    plane = (fields, cells, LANES)
    chunk = (10, 2, rows // 4, LANES)
    vmem = pl.BlockSpec(memory_space=pltpu.VMEM)
    step = pl.pallas_call(
        functools.partial(kernel, cfg),
        out_shape=jax.ShapeDtypeStruct(turned.shape, F32),
        in_specs=[vmem] * 10,
        out_specs=vmem,
        scratch_shapes=[pltpu.VMEM((fields, axial, cells + 2 * RIM, LANES), F32)]
        + [pltpu.VMEM((fields, axial, cells, LANES), F32)]
        + [pltpu.VMEM(plane, F32)] * 6
        + [pltpu.VMEM(chunk, F32)] * 5
        + [pltpu.VMEM((2, 2 * rows, 2 * LANES), BF16)]
        + [
            pltpu.SemaphoreType.DMA((2,)),
            pltpu.SemaphoreType.DMA((2,)),
            pltpu.SemaphoreType.DMA((2,)),
            pltpu.SemaphoreType.DMA((2,)),
            pltpu.SemaphoreType.DMA((2, fields)),
            pltpu.SemaphoreType.DMA((2, fields)),
            pltpu.SemaphoreType.DMA((2, 10)),
            pltpu.SemaphoreType.DMA((2, 10)),
        ],
        compiler_params=pltpu.CompilerParams(
            collective_id=0, has_side_effects=True, vmem_limit_bytes=48 * 1024 * 1024
        ),
        name="jet_section",
    )(
        turned,
        modes.reshape(1, NIN),
        jnp.asarray(cfg["top_rows"]),
        jnp.asarray(cfg["forward"]),
        jnp.asarray(cfg["inverse"]),
        jnp.asarray(cfg["place"]),
        jnp.asarray(cfg["back"]),
        jnp.asarray(cfg["ghost"]),
        jnp.asarray(cfg["turn"]),
        jnp.asarray(cfg["far"]),
    )
    return start + step.transpose(0, 1, 3, 2)


def solution(mesh):
    in_specs = (P(None, "axial", "azim", None), P(None, "axial", "azim", None), P())
    out_specs = P(None, "axial", "azim", None)
    return jax.shard_map(shards, mesh=mesh, in_specs=in_specs, out_specs=out_specs, check_vma=False)
```

time: 96.1 us -> 74.9 us (0.78); the launches traced: 94.7 us -> 74.5 us
  Pallas kernels: 81.4 us -> 64.6 us
  other arithmetic: 4.6 us -> 1.12 us
    pallas_call x1, Pallas kernels: 81.4 us -> 64.6 us  [shards(): pl.pallas_call(functools.partial(kernel, cfg), out_shape=jax.ShapeDtypeSt...]
    unnamed x15 -> x20, local copies, waits for them, and re-layouts: 4.35 us -> 8.68 us
    gather x2 -> x0, local copies, waits for them, and re-layouts: 1.39 us -> none  [the longest x1 0.7 us: shards(): counts[cfg['top']]]
    add x1 -> x0, local copies, waits for them, and re-layouts: 1.34 us -> none  [shards(): return start + step]
    gather x2 -> x0, other arithmetic: 1.33 us -> none  [the longest x1 0.67 us: shards(): counts[cfg['bottom']]]
where the time goes in v3:
time: 74.9 us; the launch traced here: 74.5 us
  Pallas kernels  64.6 us (86%)
  local copies, waits for them, and re-layouts  8.68 us (12%)
  other arithmetic  1.12 us (1%)
    pallas_call x1, Pallas kernels, shards(): pl.pallas_call(functools.partial(kernel, cfg), out_shape=jax.ShapeDtypeSt...  64.6 us
    unnamed x20, local copies, waits for them, and re-layouts  8.68 us

profile of v3, /device:TPU:0, one launch (start us, length us, event | category | flops | bytes accessed | tf_op | source)
XLA Modules:
  0.0 74.5 jit_solution(15733567117156686537)
XLA Ops:
  0.0 0.0 copy-start
  0.0 1.4 %copy-done = bf16[2,2,704,256]{3,2,1,0:T(8,128)(2,1)S(1)} copy-done((bf16[2,2,704,256]{3,2,1,0:T(8,128)(2,1)S(1)}, bf16[2,2,704,256]{3,2,1,0:T(8,128)(2,1)}, u32[]{:S(2)}) %copy-start) | copy-done | bytes 1441816
  1.4 0.0 copy-start.1
  1.4 1.2 %copy-done.1 = f32[5,2,256,96]{2,3,1,0:T(8,128)S(1)} copy-done((f32[5,2,256,96]{2,3,1,0:T(8,128)S(1)}, f32[5,2,256,96]{2,3,1,0:T(8,128)}, u32[]{:S(2)}) %copy-start.1) | copy-done | bytes 983064
  2.6 0.0 copy-start.2
  2.6 1.0 %copy-done.2 = bf16[3,256,256]{2,1,0:T(8,128)(2,1)S(1)} copy-done((bf16[3,256,256]{2,1,0:T(8,128)(2,1)S(1)}, bf16[3,256,256]{2,1,0:T(8,128)(2,1)}, u32[]{:S(2)}) %copy-start.2) | copy-done | bytes 393240
  3.6 0.0 copy-start.3
  3.6 1.0 %copy-done.3 = bf16[3,256,256]{2,1,0:T(8,128)(2,1)S(1)} copy-done((bf16[3,256,256]{2,1,0:T(8,128)(2,1)S(1)}, bf16[3,256,256]{2,1,0:T(8,128)(2,1)}, u32[]{:S(2)}) %copy-start.3) | copy-done | bytes 393240
  4.6 0.0 copy-start.4
  4.6 1.0 %copy-done.4 = f32[2,352,128]{2,1,0:T(8,128)S(1)} copy-done((f32[2,352,128]{2,1,0:T(8,128)S(1)}, f32[2,352,128]{2,1,0:T(8,128)}, u32[]{:S(2)}) %copy-start.4) | copy-done | bytes 360472
  5.5 0.0 copy-start.5
  5.5 0.9 %copy-done.5 = bf16[3,128,256]{2,1,0:T(8,128)(2,1)S(1)} copy-done((bf16[3,128,256]{2,1,0:T(8,128)(2,1)S(1)}, bf16[3,128,256]{2,1,0:T(8,128)(2,1)}, u32[]{:S(2)}) %copy-start.5) | copy-done | bytes 196632
  6.5 0.0 copy-start.6
  6.5 0.9 %copy-done.6 = bf16[2,272,64]{2,1,0:T(8,128)(2,1)S(1)} copy-done((bf16[2,272,64]{2,1,0:T(8,128)(2,1)S(1)}, bf16[2,272,64]{2,1,0:T(8,128)(2,1)}, u32[]{:S(2)}) %copy-start.6) | copy-done | bytes 69656
  7.4 0.0 copy-start.7
  7.4 0.7 copy-done.7
  8.0 0.0 copy-start.8
  8.0 0.7 copy-done.8
  8.7 0.0 copy-start.9
  8.7 64.6 %jet_section.1 = f32[5,2,96,256]{3,2,1,0:T(8,128)S(1)} custom-call(f32[5,2,96,256]{3,2,1,0:T(8,128)S(1)} %bitcast.4, s32[1,64]{1,0:T(1,128)S(1)} %bitcast.5, s32[1,128]{1,0:T(1,128)S(1)} %copy-done.8, bf16[2,2,704,256]{3,2,1,0:T(8,128)(2,1)S(1)} %copy-done, bf16[2,2,272,704]{3,2,1,0:T(8,128)(2,1)} %constant.18.clone.inverse, ...), custom_call_target="tpu_custom_call" | custom-call | tf_op jit(solution)/shard_map/jet_section/pallas_call | solution.py:495
  73.3 0.0 copy-done.9
  73.4 1.1 %bitcast_add_fusion = f32[5,2,256,96]{2,3,1,0:T(8,128)} fusion(f32[5,2,256,96]{2,3,1,0:T(8,128)S(1)} %copy-done.9, f32[5,2,96,256]{3,2,1,0:T(8,128)S(1)} %jet_section.1), kind=kLoop, calls=%fused_computation | loop fusion | flops 245760 | bytes 2949120 | tf_op jit(solution)/shard_map/add | solution.py:531
Async XLA Ops:
  0.0 1.4 %copy-start = (bf16[2,2,704,256]{3,2,1,0:T(8,128)(2,1)S(1)}, bf16[2,2,704,256]{3,2,1,0:T(8,128)(2,1)}, u32[]{:S(2)}) copy-start(bf16[2,2,704,256]{3,2,1,0:T(8,128)(2,1)} %constant.17.clone.forward) | copy-start | bytes 4325380
  1.4 1.2 %copy-start.1 = (f32[5,2,256,96]{2,3,1,0:T(8,128)S(1)}, f32[5,2,256,96]{2,3,1,0:T(8,128)}, u32[]{:S(2)}) copy-start(f32[5,2,256,96]{2,3,1,0:T(8,128)} %param.11) | copy-start | bytes 2949124
  2.6 1.0 %copy-start.2 = (bf16[3,256,256]{2,1,0:T(8,128)(2,1)S(1)}, bf16[3,256,256]{2,1,0:T(8,128)(2,1)}, u32[]{:S(2)}) copy-start(bf16[3,256,256]{2,1,0:T(8,128)(2,1)} %constant.20.clone.back) | copy-start | bytes 1179652
  3.6 1.0 %copy-start.3 = (bf16[3,256,256]{2,1,0:T(8,128)(2,1)S(1)}, bf16[3,256,256]{2,1,0:T(8,128)(2,1)}, u32[]{:S(2)}) copy-start(bf16[3,256,256]{2,1,0:T(8,128)(2,1)} %constant.19.clone.place) | copy-start | bytes 1179652
  4.6 1.0 %copy-start.4 = (f32[2,352,128]{2,1,0:T(8,128)S(1)}, f32[2,352,128]{2,1,0:T(8,128)}, u32[]{:S(2)}) copy-start(f32[2,352,128]{2,1,0:T(8,128)} %constant.22.clone.turn) | copy-start | bytes 1081348
  5.5 0.9 %copy-start.5 = (bf16[3,128,256]{2,1,0:T(8,128)(2,1)S(1)}, bf16[3,128,256]{2,1,0:T(8,128)(2,1)}, u32[]{:S(2)}) copy-start(bf16[3,128,256]{2,1,0:T(8,128)(2,1)} %constant.21.clone.ghost) | copy-start | bytes 589828
  6.5 0.9 %copy-start.6 = (bf16[2,272,64]{2,1,0:T(8,128)(2,1)S(1)}, bf16[2,272,64]{2,1,0:T(8,128)(2,1)}, u32[]{:S(2)}) copy-start(bf16[2,272,64]{2,1,0:T(8,128)(2,1)} %constant.23.clone.far_table) | copy-start | bytes 208900
  7.4 0.7 copy-start.7
  8.0 0.7 copy-start.8
  8.7 64.7 %copy-start.9 = (f32[5,2,256,96]{2,3,1,0:T(8,128)S(1)}, f32[5,2,256,96]{2,3,1,0:T(8,128)}, u32[]{:S(2)}) copy-start(f32[5,2,256,96]{2,3,1,0:T(8,128)} %param.12) | copy-start | bytes 2949124

commit v4 on v3

--- a/solution.py
+++ b/solution.py
@@ -115,12 +115,21 @@
 
 def kernel(
     cfg,
-    state, modes, bounds, forward, inverse, place, back, ghost, turn, far_table,
-    out,
-    ext, rate, outer_own, outer_left, outer_right, inner_own, inner_left, inner_right,
-    own, to_right, to_left, from_left, from_right, spectrum,
-    halo_send, halo_recv, outer_send, outer_recv, inner_send, inner_recv, wave_send, wave_recv,
+    state, modes, bounds, *refs,
 ):
+    stored, out, refs = refs[:7], refs[7], refs[8:]
+    loaded, table_sem, refs = refs[:7], refs[7], refs[8:]
+    forward, inverse, place, back, ghost, turn, far_table = loaded
+    (
+        ext, rate, outer_own, outer_left, outer_right, inner_own, inner_left, inner_right,
+        own, to_right, to_left, from_left, from_right, spectrum,
+        halo_send, halo_recv, outer_send, outer_recv, inner_send, inner_recv, wave_send, wave_recv,
+    ) = refs
+    tables = [
+        pltpu.make_async_copy(stored[k], loaded[k], table_sem.at[k]) for k in range(len(stored))
+    ]
+    for k in (2, 0, 5, 1, 3, 4, 6):
+        tables[k].start()
     rows, first_dropped = cfg["rows"], cfg["first_dropped"]
     half, quarter = rows // 2, rows // 4
     far_rows = cfg["far_rows"]
@@ -193,6 +202,7 @@
     signs = jnp.where(lane_cells >= first_dropped, parity_cells, 1.0)
     row_ids = lax.broadcasted_iota(jnp.int32, (quarter, LANES), 0)
     low_lanes = lax.broadcasted_iota(jnp.int32, (quarter, LANES), 1) < LANES // 2
+    tables[2].wait()
     top_rows = bounds[...]
     cycle_ids = lax.broadcasted_iota(jnp.int32, (8, NIN), 1)
     kept_modes = jnp.broadcast_to(modes[...], (8, NIN))
@@ -215,6 +225,7 @@
 
     for copy in halos + outers:
         copy.start()
+    tables[0].wait()
     for tile in range(3):
         high = jnp.zeros((cells, 2 * LANES), F32)
         low = jnp.zeros((cells, 2 * LANES), F32)
@@ -261,6 +272,8 @@
 
     for copy in halos:
         copy.wait()
+    for k in (5, 1, 3, 4, 6):
+        tables[k].wait()
 
     def turned(ref, c, sign):
         if c < 8:
@@ -290,20 +303,24 @@
             to_right[c, 1] = own[c, 1] + sine
             rights[c].start()
 
-    def relay(c):
-        pass_right(c, near_first)
-
-        @pl.when(jnp.logical_not(is_last))
+    def pass_left(c, when):
+        @pl.when(when & jnp.logical_not(is_last))
         def _():
             lefts[c].wait_recv()
 
-        @pl.when(inside)
+        @pl.when(when & inside)
         def _():
             cosine, sine = turned(from_right, c, -1.0)
             to_left[c, 0] = own[c, 0] + cosine
             to_left[c, 1] = own[c, 1] + sine
             lefts[c].start()
 
+    def relay_near(c):
+        pass_right(c, near_first)
+        pass_left(c, jnp.logical_not(near_first))
+
+    def relay_far(c):
+        pass_left(c, near_first)
         pass_right(c, jnp.logical_not(near_first))
 
         @pl.when(jnp.logical_not(is_first))
@@ -383,14 +400,15 @@
             for copy in inners[f]:
                 copy.start()
 
-    for c in range(5):
-        relay(c)
-    restore(0)
-    for c in range(5, 9):
-        relay(c)
-    restore(1)
-    relay(9)
-    restore(2)
+    lag = 3
+    for step in range(chunks + lag):
+        if step < chunks:
+            relay_near(step)
+        c = step - lag
+        if c >= 0:
+            relay_far(c)
+            if c in (3, 7, 9):
+                restore(c // 4)
 
     block = min(32, cells)
     deep = block + 2 * RIM
@@ -491,13 +509,17 @@
     turned = state.transpose(0, 1, 3, 2)
     plane = (fields, cells, LANES)
     chunk = (10, 2, rows // 4, LANES)
+    names = ("forward", "inverse", "place", "back", "ghost", "turn", "far")
+    tables = [jnp.asarray(cfg[name]) for name in names]
     vmem = pl.BlockSpec(memory_space=pltpu.VMEM)
     step = pl.pallas_call(
         functools.partial(kernel, cfg),
         out_shape=jax.ShapeDtypeStruct(turned.shape, F32),
-        in_specs=[vmem] * 10,
+        in_specs=[vmem] * 3 + [pl.BlockSpec(memory_space=pltpu.HBM)] * 7,
         out_specs=vmem,
-        scratch_shapes=[pltpu.VMEM((fields, axial, cells + 2 * RIM, LANES), F32)]
+        scratch_shapes=[pltpu.VMEM(table.shape, table.dtype) for table in tables]
+        + [pltpu.SemaphoreType.DMA((7,))]
+        + [pltpu.VMEM((fields, axial, cells + 2 * RIM, LANES), F32)]
         + [pltpu.VMEM((fields, axial, cells, LANES), F32)]
         + [pltpu.VMEM(plane, F32)] * 6
         + [pltpu.VMEM(chunk, F32)] * 5
@@ -520,13 +542,7 @@
         turned,
         modes.reshape(1, NIN),
         jnp.asarray(cfg["top_rows"]),
-        jnp.asarray(cfg["forward"]),
-        jnp.asarray(cfg["inverse"]),
-        jnp.asarray(cfg["place"]),
-        jnp.asarray(cfg["back"]),
-        jnp.asarray(cfg["ghost"]),
-        jnp.asarray(cfg["turn"]),
-        jnp.asarray(cfg["far"]),
+        *tables,
     )
     return start + step.transpose(0, 1, 3, 2)
 

time: 74.9 us -> 58.4 us (0.78)
  the two profiles are of different devices: /device:TPU:0 before, /device:TPU:1 now
where the time goes in v4:
time: 58.4 us; the launch traced here: 58.1 us
  Pallas kernels  48.3 us (83%)
  local copies, waits for them, and re-layouts  8.68 us (15%)
  other arithmetic  1.12 us (2%)
    pallas_call x1, Pallas kernels, shards(): pl.pallas_call(functools.partial(kernel, cfg), out_shape=jax.ShapeDtypeSt...  48.3 us
    unnamed x20, local copies, waits for them, and re-layouts  8.68 us

profile of v4, /device:TPU:1, one launch (start us, length us, event | category | flops | bytes accessed | tf_op | source)
XLA Modules:
  0.0 58.1 jit_solution(15364684678606127987)
XLA Ops:
  0.0 0.0 copy-start
  0.0 1.4 %copy-done = bf16[2,2,704,256]{3,2,1,0:T(8,128)(2,1)S(1)} copy-done((bf16[2,2,704,256]{3,2,1,0:T(8,128)(2,1)S(1)}, bf16[2,2,704,256]{3,2,1,0:T(8,128)(2,1)}, u32[]{:S(2)}) %copy-start) | copy-done | bytes 1441816
  1.4 0.0 copy-start.1
  1.4 1.2 %copy-done.1 = f32[5,2,256,96]{2,3,1,0:T(8,128)S(1)} copy-done((f32[5,2,256,96]{2,3,1,0:T(8,128)S(1)}, f32[5,2,256,96]{2,3,1,0:T(8,128)}, u32[]{:S(2)}) %copy-start.1) | copy-done | bytes 983064
  2.6 0.0 copy-start.2
  2.6 1.0 %copy-done.2 = bf16[3,256,256]{2,1,0:T(8,128)(2,1)S(1)} copy-done((bf16[3,256,256]{2,1,0:T(8,128)(2,1)S(1)}, bf16[3,256,256]{2,1,0:T(8,128)(2,1)}, u32[]{:S(2)}) %copy-start.2) | copy-done | bytes 393240
  3.6 0.0 copy-start.3
  3.6 1.0 %copy-done.3 = bf16[3,256,256]{2,1,0:T(8,128)(2,1)S(1)} copy-done((bf16[3,256,256]{2,1,0:T(8,128)(2,1)S(1)}, bf16[3,256,256]{2,1,0:T(8,128)(2,1)}, u32[]{:S(2)}) %copy-start.3) | copy-done | bytes 393240
  4.6 0.0 copy-start.4
  4.6 1.0 %copy-done.4 = f32[2,352,128]{2,1,0:T(8,128)S(1)} copy-done((f32[2,352,128]{2,1,0:T(8,128)S(1)}, f32[2,352,128]{2,1,0:T(8,128)}, u32[]{:S(2)}) %copy-start.4) | copy-done | bytes 360472
  5.5 0.0 copy-start.5
  5.5 0.9 %copy-done.5 = bf16[3,128,256]{2,1,0:T(8,128)(2,1)S(1)} copy-done((bf16[3,128,256]{2,1,0:T(8,128)(2,1)S(1)}, bf16[3,128,256]{2,1,0:T(8,128)(2,1)}, u32[]{:S(2)}) %copy-start.5) | copy-done | bytes 196632
  6.5 0.0 copy-start.6
  6.5 0.9 %copy-done.6 = bf16[2,272,64]{2,1,0:T(8,128)(2,1)S(1)} copy-done((bf16[2,272,64]{2,1,0:T(8,128)(2,1)S(1)}, bf16[2,272,64]{2,1,0:T(8,128)(2,1)}, u32[]{:S(2)}) %copy-start.6) | copy-done | bytes 69656
  7.4 0.0 copy-start.7
  7.4 0.7 %copy-done.7 = s32[64]{0:T(128)S(1)} copy-done((s32[64]{0:T(128)S(1)}, s32[64]{0:T(128)}, u32[]{:S(2)}) %copy-start.7) | copy-done | bytes 280
  8.0 0.0 copy-start.8
  8.0 0.7 %copy-done.8 = s32[1,128]{1,0:T(1,128)S(1)} copy-done((s32[1,128]{1,0:T(1,128)S(1)}, s32[1,128]{1,0:T(1,128)}, u32[]{:S(2)}) %copy-start.8) | copy-done | bytes 536
  8.7 0.0 copy-start.9
  8.7 48.3 %jet_section.1 = f32[5,2,96,256]{3,2,1,0:T(8,128)S(1)} custom-call(f32[5,2,96,256]{3,2,1,0:T(8,128)S(1)} %bitcast.4, s32[1,64]{1,0:T(1,128)S(1)} %bitcast.5, s32[1,128]{1,0:T(1,128)S(1)} %copy-done.8, bf16[2,2,704,256]{3,2,1,0:T(8,128)(2,1)S(1)} %copy-done, bf16[2,2,272,704]{3,2,1,0:T(8,128)(2,1)} %constant.17.clone.refs_1_, ...), custom_call_target="tpu_custom_call" | custom-call | tf_op jit(solution)/shard_map/jet_section/pallas_call | solution.py:515
  57.0 0.0 copy-done.9
  57.0 1.1 %bitcast_add_fusion = f32[5,2,256,96]{2,3,1,0:T(8,128)} fusion(f32[5,2,256,96]{2,3,1,0:T(8,128)S(1)} %copy-done.9, f32[5,2,96,256]{3,2,1,0:T(8,128)S(1)} %jet_section.1), kind=kLoop, calls=%fused_computation | loop fusion | flops 245760 | bytes 2949120 | tf_op jit(solution)/shard_map/add | solution.py:547
Async XLA Ops:
  0.0 1.4 %copy-start = (bf16[2,2,704,256]{3,2,1,0:T(8,128)(2,1)S(1)}, bf16[2,2,704,256]{3,2,1,0:T(8,128)(2,1)}, u32[]{:S(2)}) copy-start(bf16[2,2,704,256]{3,2,1,0:T(8,128)(2,1)} %constant.16.clone.refs_0_) | copy-start | bytes 4325380
  1.4 1.2 %copy-start.1 = (f32[5,2,256,96]{2,3,1,0:T(8,128)S(1)}, f32[5,2,256,96]{2,3,1,0:T(8,128)}, u32[]{:S(2)}) copy-start(f32[5,2,256,96]{2,3,1,0:T(8,128)} %param.11) | copy-start | bytes 2949124
  2.6 1.0 %copy-start.2 = (bf16[3,256,256]{2,1,0:T(8,128)(2,1)S(1)}, bf16[3,256,256]{2,1,0:T(8,128)(2,1)}, u32[]{:S(2)}) copy-start(bf16[3,256,256]{2,1,0:T(8,128)(2,1)} %constant.19.clone.refs_3_) | copy-start | bytes 1179652
  3.6 1.0 %copy-start.3 = (bf16[3,256,256]{2,1,0:T(8,128)(2,1)S(1)}, bf16[3,256,256]{2,1,0:T(8,128)(2,1)}, u32[]{:S(2)}) copy-start(bf16[3,256,256]{2,1,0:T(8,128)(2,1)} %constant.18.clone.refs_2_) | copy-start | bytes 1179652
  4.6 1.0 %copy-start.4 = (f32[2,352,128]{2,1,0:T(8,128)S(1)}, f32[2,352,128]{2,1,0:T(8,128)}, u32[]{:S(2)}) copy-start(f32[2,352,128]{2,1,0:T(8,128)} %constant.21.clone.refs_5_) | copy-start | bytes 1081348
  5.5 0.9 %copy-start.5 = (bf16[3,128,256]{2,1,0:T(8,128)(2,1)S(1)}, bf16[3,128,256]{2,1,0:T(8,128)(2,1)}, u32[]{:S(2)}) copy-start(bf16[3,128,256]{2,1,0:T(8,128)(2,1)} %constant.20.clone.refs_4_) | copy-start | bytes 589828
  6.5 0.9 %copy-start.6 = (bf16[2,272,64]{2,1,0:T(8,128)(2,1)S(1)}, bf16[2,272,64]{2,1,0:T(8,128)(2,1)}, u32[]{:S(2)}) copy-start(bf16[2,272,64]{2,1,0:T(8,128)(2,1)} %constant.22.clone.refs_6_) | copy-start | bytes 208900
  7.4 0.7 %copy-start.7 = (s32[64]{0:T(128)S(1)}, s32[64]{0:T(128)}, u32[]{:S(2)}) copy-start(s32[64]{0:T(128)} %param.13) | copy-start | bytes 772
  8.0 0.7 %copy-start.8 = (s32[1,128]{1,0:T(1,128)S(1)}, s32[1,128]{1,0:T(1,128)}, u32[]{:S(2)}) copy-start(s32[1,128]{1,0:T(1,128)} %constant.23.clone.bounds) | copy-start | bytes 1540
  8.7 48.3 %copy-start.9 = (f32[5,2,256,96]{2,3,1,0:T(8,128)S(1)}, f32[5,2,256,96]{2,3,1,0:T(8,128)}, u32[]{:S(2)}) copy-start(f32[5,2,256,96]{2,3,1,0:T(8,128)} %param.12) | copy-start | bytes 2949124
